TPU v7x, 32 devices: a whole 2x2x4 slice. The times are simulated.
32 devices in a mesh: grp: 2 (over x), tok: 16 (over z, y, core).
Axes of the slice: x: 2, y: 2, z: 4, core: 2. Of those that a mesh axis runs over, the one named last changes fastest.
Arguments:
- keys: bfloat16 [4096, 1024], P(('grp', 'tok')), parts along dimension 0, may hold values from -6 to 6
- values: bfloat16 [4096, 1024], P(('grp', 'tok')), parts along dimension 0, may hold values from -6 to 6
- queries: bfloat16 [4096, 1024], P(('grp', 'tok')), parts along dimension 0, may hold values from -6 to 6
- rates: float32 [2, 4096], P(None, ('grp', 'tok')), parts along dimension 1, may hold values from 0.3 to 3
- fast_weights: bfloat16 [2, 3, 512, 512], replicated, may hold values from -0.25 to 0.25
Outputs:
- readout: bfloat16 [4096, 1024], P(('grp', 'tok')), parts along dimension 0
- new_weights: bfloat16 [4, 3, 512, 512], P('grp'), parts along dimension 0
There are 2 independent parts, one for each index of `grp`. A program takes and returns all parts, laid end to end along the dimension named above; an argument that names none is the same for every part. Nothing has to cross between parts.
All inputs are finite; a program needn't handle non-finite values.
Results may differ from a plain program's by a relative error of at most 0.017.
Values may be sent and summed in bfloat16 or wider, within the bound.
A program may use at most 64 MiB of HBM per device.

v0:
```python
import functools

import jax
import jax.numpy as jnp
from jax import lax
from jax.experimental import pallas as pl
from jax.experimental.pallas import tpu as pltpu
from jax.sharding import PartitionSpec as P

HEADS = 2
NS_STEPS = 2
CHUNKS = 8
SUM_CHUNKS = 8
HALVES = 2
CROSS = 2
SUM_LAG = 3
LAG = 4
BOTH = 4
SHIFT = 0
MESH = pl.DeviceIdType.MESH
F32 = jnp.float32
BF16 = jnp.bfloat16


def dot(a, b):
    return jnp.dot(a, b, preferred_element_type=F32)


def dot_nt(a, b):
    return lax.dot_general(a, b, (((1,), (1,)), ((), ())), preferred_element_type=F32)


def dot_tn(a, b):
    return lax.dot_general(a, b, (((0,), (0,)), ((), ())), preferred_element_type=F32)


def kernel(
    Z, Y,
    k_hbm, v_hbm, q_hbm, r_hbm, w_hbm,
    out_ref, neww_ref,
    v_ref, q_ref, r_ref, w_ref,
    o_loc, left, right, recv, sendbuf, m_buf, x_buf, g_buf, wn, recv_y,
    tok_send, tok_recv, chain_send, chain_recv, cross_recv, w_send, w_recv, out_sem, in_sem,
):
    tokens = k_hbm.shape[0]
    D = w_ref.shape[2]
    R = D // CHUNKS
    RS = D * HALVES // SUM_CHUNKS
    CS = D // HALVES
    PEERS = 2 * Y
    me = lax.axis_index("tok")
    c = me % 2
    y = (me // 2) % Y
    z = me // PEERS
    mine = y * 2 + c
    mid = Z // 2 - 1

    def at(zz, yy, cc):
        return {"tok": (zz * Y + yy) * 2 + cc}

    own_rows = pl.ds(pl.multiple_of(mine * tokens, tokens), tokens)
    own_cols = pl.ds(pl.multiple_of(c * D, D), D)
    loads = [
        pltpu.make_async_copy(src, dst, in_sem.at[n])
        for n, (src, dst) in enumerate((
            (r_hbm, r_ref), (v_hbm, v_ref), (k_hbm.at[:, own_cols], left.at[0, own_rows, :]),
            (w_hbm.at[c], w_ref.at[c]), (q_hbm, q_ref),
        ))
    ]
    for load in loads:
        load.start()

    barrier = pltpu.get_barrier_semaphore()
    for d in range(1, PEERS):
        peer = z * PEERS + (mine + d) % PEERS
        pl.semaphore_signal(barrier, inc=1, device_id={"tok": peer}, device_id_type=MESH)

    @pl.when(z > 0)
    def _():
        pl.semaphore_signal(barrier, inc=1, device_id={"tok": me - PEERS}, device_id_type=MESH)

    @pl.when(z < Z - 1)
    def _():
        pl.semaphore_signal(barrier, inc=1, device_id={"tok": me + PEERS}, device_id_type=MESH)

    loads[0].wait()
    loads[1].wait()
    for h in range(HEADS):
        row = jnp.broadcast_to(r_ref[h : h + 1, :], (128, tokens))
        col = jnp.concatenate([row.T] * (D // 128), axis=1)
        o_loc[h] = (-col * v_ref[:, h * D : (h + 1) * D].astype(F32)).astype(BF16)

    right[2, own_rows, :] = o_loc[c]

    pl.semaphore_wait(
        barrier, (PEERS - 1) + jnp.where(z > 0, 1, 0) + jnp.where(z < Z - 1, 1, 0)
    )

    def token_copies(d):
        p = (mine + d) % PEERS
        cc = p % 2
        dev = {"tok": z * PEERS + p}
        cols = pl.ds(pl.multiple_of(cc * D, D), D)
        return (
            pltpu.make_async_remote_copy(
                k_hbm.at[:, cols], left.at[0, own_rows, :],
                tok_send.at[0, d - 1], tok_recv.at[0, d - 1],
                device_id=dev, device_id_type=MESH),
            pltpu.make_async_remote_copy(
                o_loc.at[cc], right.at[2, own_rows, :],
                tok_send.at[1, d - 1], tok_recv.at[1, d - 1],
                device_id=dev, device_id_type=MESH),
        )

    def reached(d):
        p = (mine + d) % PEERS
        return jnp.logical_or(p % 2 != CROSS, p // 2 == y)

    for d in range(1, PEERS):

        @pl.when(reached(d))
        def _():
            for cp in token_copies(d):
                cp.start()

    loads[2].wait()
    loads[3].wait()

    def forward_block(d, _):
        p = (mine + PEERS - d) % PEERS

        @pl.when(jnp.logical_or(c != CROSS, p // 2 == y))
        def _():
            forward_rows(d, p)

        return 0

    def forward_rows(d, p):
        @pl.when(d > 0)
        def _():
            for cp in token_copies(d):
                cp.wait_recv()

        rows = pl.ds(pl.multiple_of(p * tokens, tokens), tokens)
        key = left[0, rows, :]
        gate = dot(key, w_ref[c, 0])
        upper = dot(key, w_ref[c, 1])
        back = dot_nt(right[2, rows, :], w_ref[c, 2])
        sigma = jax.nn.sigmoid(gate)
        silu_gate = gate * sigma
        left[1, rows, :] = (silu_gate * upper).astype(BF16)
        right[0, rows, :] = (back * upper * sigma * (1.0 + gate * (1.0 - sigma))).astype(BF16)
        right[1, rows, :] = (back * silu_gate).astype(BF16)

    lax.fori_loop(0, PEERS, forward_block, 0)

    def place(w, h):
        col = jnp.where(w + h >= 2, 1, 0)
        own = jnp.where(
            col == h,
            jnp.where(w == h, 0, Z - 1),
            mid + SHIFT * col,
        )
        return col, own

    def crosses(w):
        return jnp.logical_and(c == CROSS, y != place(w, c)[0])

    def active(w):
        return jnp.logical_or(c == CROSS, y == place(w, c)[0])

    def owns(w):
        col, own = place(w, c)
        return jnp.logical_and(y == col, z == own)

    is_owner = functools.reduce(jnp.logical_or, [owns(w) for w in range(3)])
    owned_w = jnp.where(owns(0), 0, jnp.where(owns(1), 1, 2))

    def chain_copy(w, i, step, side):
        return pltpu.make_async_remote_copy(
            sendbuf.at[w, i], recv.at[side, w, i],
            chain_send.at[w, i], chain_recv.at[side, w, i],
            device_id={"tok": me + step * PEERS}, device_id_type=MESH)

    def cross_copy(w, i, slot):
        return pltpu.make_async_remote_copy(
            sendbuf.at[w, i], recv_y.at[slot, i],
            chain_send.at[w, i], cross_recv.at[slot, i],
            device_id=at(z, place(w, c)[0], c), device_id_type=MESH)

    def take(side, w, i):
        chain_copy(w, i, 1, side).wait_recv()
        part[...] += recv[side, w, i].astype(F32)

    part = x_buf.at[0, pl.ds(0, RS), pl.ds(0, CS)]
    chip_rows = pl.ds(pl.multiple_of(y * 2 * tokens, 2 * tokens), 2 * tokens)

    def reduce_event(w, i):
        col, own = place(w, c)
        rows = pl.ds(pl.multiple_of((i // HALVES) * RS, RS), RS)
        cols = pl.ds(pl.multiple_of((i % HALVES) * CS, CS), CS)
        side_l = 1 if w == 2 else 0

        @pl.when(c != CROSS)
        def _():
            part[...] = dot_tn(left[side_l, :, rows], right[w, :, cols])

        @pl.when(c == CROSS)
        def _():
            part[...] = dot_tn(left[side_l, chip_rows, rows], right[w, chip_rows, cols])

        @pl.when(jnp.logical_and(z > 0, z <= own))
        def _():
            take(0, w, i)

        @pl.when(jnp.logical_and(z < Z - 1, z >= own))
        def _():
            take(1, w, i)

        @pl.when(owns(w))
        def _():
            @pl.when(c == CROSS)
            def _():
                for slot in range(Y - 1):
                    cross_copy(w, i, slot).wait_recv()
                    part[...] += recv_y[slot, i].astype(F32)

            m_buf[rows, cols] = part[...].astype(BF16)

        @pl.when(jnp.logical_not(owns(w)))
        def _():
            sendbuf[w, i] = part[...].astype(BF16)

        @pl.when(z < own)
        def _():
            chain_copy(w, i, 1, 0).start()

        @pl.when(z > own)
        def _():
            chain_copy(w, i, -1, 1).start()

        @pl.when(jnp.logical_and(z == own, crosses(w)))
        def _():
            cross_copy(w, i, (y + Y - col) % Y - 1).start()

    def depth(w):
        own = place(w, c)[1]
        rise = jnp.where(z <= own, z, 0)
        fall = jnp.where(z >= own, Z - 1 - z, 0)
        met = jnp.where(jnp.logical_and(owns(w), c == CROSS), 1, 0)
        return SUM_LAG * (jnp.maximum(rise, fall) + met)

    def reduce_step(t, _):
        for w in range(3):
            i = t - depth(w)

            @pl.when(jnp.logical_and(active(w), jnp.logical_and(i >= 0, i < SUM_CHUNKS)))
            def _():
                reduce_event(w, i)

        return 0

    lax.fori_loop(0, SUM_CHUNKS + SUM_LAG * Z, reduce_step, 0)

    def w_copies(w, i, go):
        col, own = place(w, c)
        rows = pl.ds(pl.multiple_of(i * R, R), R)
        block = wn.at[c, w, rows, :]
        in_col = y == col
        both = i % BOTH == BOTH - 1
        along = jnp.logical_or(in_col, both)

        def copy(kind, dev):
            cp = pltpu.make_async_remote_copy(
                block, block, w_send.at[w, i, kind], w_recv.at[c, w, i],
                device_id=dev, device_id_type=MESH)
            cp.start() if go else cp.wait_send()

        @pl.when(jnp.logical_and(along, jnp.logical_and(z >= own, z < Z - 1)))
        def _():
            copy(0, {"tok": me + PEERS})

        @pl.when(jnp.logical_and(along, jnp.logical_and(z <= own, z > 0)))
        def _():
            copy(1, {"tok": me - PEERS})

        @pl.when(jnp.logical_and(in_col, jnp.logical_or(jnp.logical_not(both), z == own)))
        def _():
            for dy in range(1, Y):
                copy(2 + dy, at(z, (y + dy) % Y, c))

        copy(2, at(z, y, 1 - c))

    def wait_block(h, w, i):
        rows = pl.ds(pl.multiple_of(i * R, R), R)
        block = wn.at[h, w, rows, :]
        pltpu.make_async_remote_copy(
            block, block, w_send.at[w, i, 2], w_recv.at[h, w, i],
            device_id=at(z, y, 1 - c), device_id_type=MESH).wait_recv()

    @pl.when(is_owner)
    def _():
        wide = m_buf[...].astype(F32)
        norm = jnp.sqrt(jnp.sum(wide * wide)) + 1e-07
        m_buf[...] = (wide / norm).astype(BF16)
        for step in range(NS_STEPS):
            x = m_buf[...]
            g_buf[...] = dot_nt(x, x).astype(BF16)
            g = g_buf[...]
            mixed = (-4.775 * g.astype(F32) + 2.0315 * dot(g, g)).astype(BF16)
            x_buf[0] = 3.4445 * x.astype(F32) + dot(mixed, x)
            m_buf[...] = x_buf[0].astype(BF16)
        for i in range(CHUNKS):
            rows = slice(i * R, (i + 1) * R)
            old = w_ref[c, owned_w, rows, :].astype(F32)
            fresh = old - m_buf[rows, :].astype(F32)
            scale = jnp.sqrt(
                (jnp.mean(old * old, axis=1, keepdims=True) + 1e-06)
                / (jnp.mean(fresh * fresh, axis=1, keepdims=True) + 1e-06)
            )
            wn[c, owned_w, rows, :] = (fresh * scale).astype(BF16)
            w_copies(owned_w, i, True)

    def spread(t, _):
        for n in range(3):
            w = jnp.where(z < Z // 2, n, 2 - n)
            col, own = place(w, c)
            hops = jnp.abs(z - own) + jnp.where(y == col, 0, 1)
            i = t - LAG * (hops - 1)

            @pl.when(jnp.logical_and(hops > 0, jnp.logical_and(i >= 0, i < CHUNKS)))
            def _():
                wait_block(c, w, i)
                w_copies(w, i, True)

        return 0

    lax.fori_loop(0, CHUNKS + LAG * (Z - 1), spread, 0)

    def apply(h):
        cols = pl.ds(pl.multiple_of(h * D, D), D)
        query = q_ref[:, cols]
        gate = dot(query, wn[h, 0])
        upper = dot(query, wn[h, 1])
        hidden = (gate * jax.nn.sigmoid(gate) * upper).astype(BF16)
        out_ref[:, cols] = dot(hidden, wn[h, 2]).astype(BF16)

    def save(h, at_sem):
        return pltpu.make_async_copy(wn.at[h], neww_ref.at[h], out_sem.at[at_sem])

    save(c, 0).start()

    def turn(s, _):
        @pl.when(s == 1)
        def _():
            def wait_all(i, _):
                for w in range(3):
                    wait_block(1 - c, w, i)
                return 0

            lax.fori_loop(0, CHUNKS, wait_all, 0)
            save(1 - c, 1).start()

        apply(jnp.where(s == 0, c, 1 - c))
        return 0

    loads[4].wait()
    lax.fori_loop(0, 2, turn, 0)

    for d in range(1, PEERS):

        @pl.when(reached(d))
        def _():
            for cp in token_copies(d):
                cp.wait_send()

    def drain_sums(i, _):
        for w in range(3):

            @pl.when(jnp.logical_and(active(w), jnp.logical_not(owns(w))))
            def _():
                chain_copy(w, i, 1, 0).wait_send()

        return 0

    lax.fori_loop(0, SUM_CHUNKS, drain_sums, 0)

    def drain(i, _):
        for w in range(3):
            w_copies(w, i, False)
        return 0

    lax.fori_loop(0, CHUNKS, drain, 0)
    save(c, 0).wait()
    save(1 - c, 1).wait()


def store(a_ref, b_ref, a_out, b_out, sem):
    copies = [
        pltpu.make_async_copy(b_ref, b_out, sem.at[0]),
        pltpu.make_async_copy(a_ref, a_out, sem.at[1]),
    ]
    for cp in copies:
        cp.start()
    for cp in copies:
        cp.wait()


def body(Z, Y, keys, values, queries, rates, fast_weights):
    D = fast_weights.shape[2]
    tokens = keys.shape[0]
    rows = tokens * 2 * Y
    vmem = pl.BlockSpec(memory_space=pltpu.VMEM)
    hbm = pl.BlockSpec(memory_space=pltpu.MemorySpace.HBM)

    def run(*refs):
        kernel(Z, Y, *refs)

    out, fresh = pl.pallas_call(
        run,
        out_shape=(
            jax.ShapeDtypeStruct((tokens, HEADS * D), BF16),
            jax.ShapeDtypeStruct((HEADS, 3, D, D), BF16),
        ),
        in_specs=[hbm] * 5,
        out_specs=(vmem, pl.BlockSpec(memory_space=pl.ANY)),
        scratch_shapes=[
            pltpu.VMEM((tokens, HEADS * D), BF16),
            pltpu.VMEM((tokens, HEADS * D), BF16),
            pltpu.VMEM(rates.shape, F32),
            pltpu.VMEM((HEADS, 3, D, D), BF16),
            pltpu.VMEM((HEADS, tokens, D), BF16),
            pltpu.VMEM((2, rows, D), BF16),
            pltpu.VMEM((3, rows, D), BF16),
            pltpu.VMEM((2, 3, SUM_CHUNKS, D * HALVES // SUM_CHUNKS, D // HALVES), BF16),
            pltpu.VMEM((3, SUM_CHUNKS, D * HALVES // SUM_CHUNKS, D // HALVES), BF16),
            pltpu.VMEM((D, D), BF16),
            pltpu.VMEM((1, D, D), F32),
            pltpu.VMEM((D, D), BF16),
            pltpu.VMEM((HEADS, 3, D, D), BF16),
            pltpu.VMEM((Y - 1, SUM_CHUNKS, D * HALVES // SUM_CHUNKS, D // HALVES), BF16),
            pltpu.SemaphoreType.DMA((2, 2 * Y - 1)),
            pltpu.SemaphoreType.DMA((2, 2 * Y - 1)),
            pltpu.SemaphoreType.DMA((3, SUM_CHUNKS)),
            pltpu.SemaphoreType.DMA((2, 3, SUM_CHUNKS)),
            pltpu.SemaphoreType.DMA((Y - 1, SUM_CHUNKS)),
            pltpu.SemaphoreType.DMA((3, CHUNKS, 2 + Y)),
            pltpu.SemaphoreType.DMA((HEADS, 3, CHUNKS)),
            pltpu.SemaphoreType.DMA((2,)),
            pltpu.SemaphoreType.DMA((5,)),
        ],
        compiler_params=pltpu.CompilerParams(
            collective_id=0, has_side_effects=True, vmem_limit_bytes=30 * 1024 * 1024
        ),
        name="ttt_step",
    )(*[pltpu.with_memory_space_constraint(a, pltpu.MemorySpace.HBM) for a in (keys, values, queries, rates, fast_weights)])
    anywhere = pl.BlockSpec(memory_space=pl.ANY)
    return pl.pallas_call(
        store,
        out_shape=(
            jax.ShapeDtypeStruct(out.shape, BF16),
            jax.ShapeDtypeStruct(fresh.shape, BF16),
        ),
        in_specs=[anywhere] * 2,
        out_specs=(hbm, hbm),
        scratch_shapes=[pltpu.SemaphoreType.DMA((2,))],
        compiler_params=pltpu.CompilerParams(vmem_limit_bytes=1024 * 1024),
        name="store",
    )(out, fresh)


def solution(mesh):
    chips = mesh.shape["tok"] // 2
    Y = 1
    while Y * Y * 4 <= chips and chips % (2 * Y) == 0:
        Y *= 2
    Z = chips // Y
    return jax.shard_map(
        functools.partial(body, Z, Y),
        mesh=mesh,
        in_specs=(
            P(("grp", "tok"), None),
            P(("grp", "tok"), None),
            P(("grp", "tok"), None),
            P(None, ("grp", "tok")),
            P(),
        ),
        out_specs=(P(("grp", "tok"), None), P("grp", None, None, None)),
        check_vma=False,
    )
```

profile of v0, /device:TPU:0, one launch (start us, length us, event | category | flops | bytes accessed | tf_op | source)
XLA Modules:
  0.0 61.8 jit_solution(9811598124246910274)
XLA Ops:
  0.6 59.4 %ttt_step.1 = (bf16[128,1024]{1,0:T(8,128)(2,1)S(1)}, bf16[2,3,512,512]{3,2,1,0:T(8,128)(2,1)S(1)}) custom-call(bf16[128,1024]{1,0:T(8,128)(2,1)} %refs_0_.1, bf16[128,1024]{1,0:T(8,128)(2,1)} %refs_1_.1, bf16[128,1024]{1,0:T(8,128)(2,1)} %refs_2_.1, f32[2,128]{1,0:T(2,128)} %refs_3_.1, bf16[2,3,512,512]{3,2,1,0:T(8,128)(2,1)} %refs_4_.1), custom_call_target="tpu_custom_call" | custom-call | tf_op jit(solution)/shard_map/ttt_step/pallas_call | solution.py:419
  60.0 1.8 %store.1 = (bf16[128,1024]{1,0:T(8,128)(2,1)}, bf16[2,3,512,512]{3,2,1,0:T(8,128)(2,1)}) custom-call(bf16[128,1024]{1,0:T(8,128)(2,1)S(1)} %get-tuple-element.4.a_ref, bf16[2,3,512,512]{3,2,1,0:T(8,128)(2,1)S(1)} %get-tuple-element.5.b_ref), custom_call_target="tpu_custom_call" | custom-call | tf_op jit(solution)/shard_map/store/pallas_call | solution.py:458
where the time goes:
time: 62.1 us; the launch traced here: 61.8 us
  Pallas kernels  61.1 us (98%)
  between operations  0.64 us (1%)
    pallas_call x1, Pallas kernels, body(): pl.pallas_call(run, out_shape=(jax.ShapeDtypeStruct((tokens, HEADS * D),...  59.4 us
    pallas_call x1, Pallas kernels, body(): pl.pallas_call(store, out_shape=(jax.ShapeDtypeStruct(out.shape, BF16), j...  1.76 us

commit v1 on v0

v1 whole, which is shorter than its diff:
```python
import functools

import jax
import jax.numpy as jnp
from jax import lax
from jax.experimental import pallas as pl
from jax.experimental.pallas import tpu as pltpu
from jax.sharding import PartitionSpec as P

HEADS = 2
NS_STEPS = 2
CHUNKS = 8
SUM_COLS = 256
SUM_ROWS = 128
PIECES = 2
SUM_LAG = 2
SUM_WAVE = 4
LAG = 4
WAVE = 4
BOTH = 4
SHIFT = 0
MESH = pl.DeviceIdType.MESH
F32 = jnp.float32
BF16 = jnp.bfloat16


def dot(a, b):
    return jnp.dot(a, b, preferred_element_type=F32)


def dot_nt(a, b):
    return lax.dot_general(a, b, (((1,), (1,)), ((), ())), preferred_element_type=F32)


def dot_tn(a, b):
    return lax.dot_general(a, b, (((0,), (0,)), ((), ())), preferred_element_type=F32)


def kernel(
    Z,
    k_hbm, v_hbm, q_hbm, r_hbm, w_hbm,
    out_ref, neww_ref,
    v_ref, q_ref, r_ref, w_ref,
    o_loc, keys, outer, grads, recv, sendbuf, part, m_buf, x_buf, g_buf, wn, hid,
    tok_send, tok_recv, chain_send, chain_recv, m_recv, w_send, w_recv, out_sem, in_sem,
):
    tokens = k_hbm.shape[0]
    D = w_ref.shape[1]
    half = D // 2
    R = D // CHUNKS
    SUM_CHUNKS = D * half // (SUM_ROWS * SUM_COLS)
    piece = tokens // PIECES
    me = lax.axis_index("tok")
    c = me % 2
    y = (me // 2) % 2
    z = me // 4

    def mid(h):
        return Z // 2 - 1 + SHIFT * h

    def at(zz, yy, cc):
        return {"tok": (zz * 2 + yy) * 2 + cc}

    def block_rows(p, j, n):
        return pl.ds(pl.multiple_of(p * tokens + j * n, n), n)

    def head_cols(h):
        return pl.ds(pl.multiple_of(h * D, D), D)

    sibling = at(z, y, 1 - c)
    across = at(z, 1 - y, c)
    mine = y * 2 + c
    other = (1 - y) * 2 + c
    half_cols = pl.ds(pl.multiple_of(c * half, half), half)

    loads = [
        pltpu.make_async_copy(src, dst, in_sem.at[n])
        for n, (src, dst) in enumerate((
            (r_hbm, r_ref), (v_hbm, v_ref),
            (k_hbm.at[:, head_cols(y)], keys.at[block_rows(mine, 0, tokens), :]),
            (w_hbm.at[y], w_ref), (q_hbm, q_ref),
        ))
    ]
    for load in loads:
        load.start()

    barrier = pltpu.get_barrier_semaphore()
    for peer in (sibling, across):
        pl.semaphore_signal(barrier, inc=1, device_id=peer, device_id_type=MESH)

    @pl.when(z > 0)
    def _():
        pl.semaphore_signal(barrier, inc=1, device_id={"tok": me - 4}, device_id_type=MESH)

    @pl.when(z < Z - 1)
    def _():
        pl.semaphore_signal(barrier, inc=1, device_id={"tok": me + 4}, device_id_type=MESH)

    loads[0].wait()
    loads[1].wait()
    for h in range(HEADS):
        row = jnp.broadcast_to(r_ref[h : h + 1, :], (128, tokens))
        col = jnp.concatenate([row.T] * (D // 128), axis=1)
        o_loc[h] = (-col * v_ref[:, h * D : (h + 1) * D].astype(F32)).astype(BF16)

    outer[block_rows(mine, 0, tokens), :] = o_loc[y]

    pl.semaphore_wait(barrier, 2 + jnp.where(z > 0, 1, 0) + jnp.where(z < Z - 1, 1, 0))

    def token_copy(a, j, kind):
        rows = slice(j * piece, (j + 1) * piece)
        held = (keys, outer)[a]
        if kind == 2:
            block = held.at[block_rows(other, j, piece), :]
            return pltpu.make_async_remote_copy(
                block, block, tok_send.at[a, kind, j], tok_recv.at[a, other, j],
                device_id=sibling, device_id_type=MESH)
        h = y if kind == 0 else 1 - y
        src = o_loc.at[h, rows, :] if a else k_hbm.at[rows, head_cols(h)]
        return pltpu.make_async_remote_copy(
            src, held.at[block_rows(mine, j, piece), :],
            tok_send.at[a, kind, j], tok_recv.at[a, mine, j],
            device_id=across if kind else sibling, device_id_type=MESH)

    for a in range(2):
        for kind in (1, 0):
            for j in range(PIECES):
                token_copy(a, j, kind).start()

    loads[2].wait()
    loads[3].wait()

    def forward_block(d, _):
        p = jnp.where(d < 2, y, 1 - y) * 2 + jnp.where(d % 2 == 0, c, 1 - c)

        @pl.when(d > 0)
        def _():
            for a in range(2):
                for j in range(PIECES):
                    block = (keys, outer)[a].at[block_rows(p, j, piece), :]
                    pltpu.make_async_remote_copy(
                        block, block, tok_send.at[a, 0, j], tok_recv.at[a, p, j],
                        device_id=sibling, device_id_type=MESH).wait_recv()

                    @pl.when(d == 2)
                    def _():
                        token_copy(a, j, 2).start()

        rows = block_rows(p, 0, tokens)
        key = keys[rows, :]
        gate = dot(key, w_ref[0, :, half_cols])
        upper = dot(key, w_ref[1, :, half_cols])
        back = dot_nt(outer[rows, :], w_ref[2, half_cols, :])
        sigma = jax.nn.sigmoid(gate)
        silu_gate = gate * sigma
        grads[2, rows, :] = (silu_gate * upper).astype(BF16)
        grads[0, rows, :] = (back * upper * sigma * (1.0 + gate * (1.0 - sigma))).astype(BF16)
        grads[1, rows, :] = (back * silu_gate).astype(BF16)
        return 0

    lax.fori_loop(0, 4, forward_block, 0)

    def owner_z(w, h):
        return (0, Z - 1, mid(h))[w]

    def owner_core(w, h):
        return h if w < 2 else 1 - h

    def chain_copy(w, i, step, side):
        return pltpu.make_async_remote_copy(
            sendbuf.at[w, i], recv.at[side, w, i],
            chain_send.at[w, i], chain_recv.at[side, w, i],
            device_id={"tok": me + step * 4}, device_id_type=MESH)

    def place(w, i):
        across_cols = (half if w < 2 else D) // SUM_COLS
        r = i // across_cols
        q = i % across_cols
        base_r = 0 if w < 2 else c * half
        base_q = c * half if w < 2 else 0
        return (
            pl.ds(pl.multiple_of(r * SUM_ROWS, SUM_ROWS), SUM_ROWS),
            pl.ds(pl.multiple_of(q * SUM_COLS, SUM_COLS), SUM_COLS),
            pl.ds(pl.multiple_of(base_r + r * SUM_ROWS, SUM_ROWS), SUM_ROWS),
            pl.ds(pl.multiple_of(base_q + q * SUM_COLS, SUM_COLS), SUM_COLS),
        )

    def hand_over(w, i):
        _, _, rows, cols = place(w, i)
        return pltpu.make_async_remote_copy(
            sendbuf.at[w, i], m_buf.at[rows, cols], chain_send.at[w, i], m_recv.at[i],
            device_id=sibling, device_id_type=MESH)

    def take(side, w, i):
        chain_copy(w, i, 1, side).wait_recv()
        part[...] += recv[side, w, i].astype(F32)

    def reduce_event(w, i):
        own = owner_z(w, y)
        keeps = jnp.logical_and(z == own, c == owner_core(w, y))
        left_cols, right_cols, rows, cols = place(w, i)
        if w < 2:
            part[...] = dot_tn(keys[:, left_cols], grads[w, :, right_cols])
        else:
            part[...] = dot_tn(grads[2, :, left_cols], outer[:, right_cols])

        @pl.when(jnp.logical_and(z > 0, z <= own))
        def _():
            take(0, w, i)

        @pl.when(jnp.logical_and(z < Z - 1, z >= own))
        def _():
            take(1, w, i)

        @pl.when(keeps)
        def _():
            m_buf[rows, cols] = part[...].astype(BF16)

        @pl.when(jnp.logical_not(keeps))
        def _():
            sendbuf[w, i] = part[...].astype(BF16)

        @pl.when(z < own)
        def _():
            chain_copy(w, i, 1, 0).start()

        @pl.when(z > own)
        def _():
            chain_copy(w, i, -1, 1).start()

        @pl.when(jnp.logical_and(z == own, jnp.logical_not(keeps)))
        def _():
            hand_over(w, i).start()

    def depth(w):
        own = owner_z(w, y)
        rise = jnp.where(z <= own, z, 0)
        fall = jnp.where(z >= own, Z - 1 - z, 0)
        return SUM_LAG * jnp.maximum(rise, fall) + (SUM_WAVE if w == 2 else 0)

    def reduce_step(t, _):
        for w in range(3):
            i = t - depth(w)

            @pl.when(jnp.logical_and(i >= 0, i < SUM_CHUNKS))
            def _():
                reduce_event(w, i)

        return 0

    lax.fori_loop(0, SUM_CHUNKS + SUM_WAVE + SUM_LAG * (Z - 1), reduce_step, 0)

    def stream_head(w):
        return c if w < 2 else 1 - c

    def owns(w):
        h = stream_head(w)
        return jnp.logical_and(y == h, z == owner_z(w, h))

    def w_copies(w, i, go):
        h = stream_head(w)
        own = owner_z(w, h)
        rows = pl.ds(pl.multiple_of(i * R, R), R)
        block = wn.at[h, w, rows, :]
        in_col = y == h
        both = i % BOTH == BOTH - 1
        along = jnp.logical_or(in_col, both)

        def copy(kind, dev):
            cp = pltpu.make_async_remote_copy(
                block, block, w_send.at[w, i, kind], w_recv.at[h, w, i],
                device_id=dev, device_id_type=MESH)
            cp.start() if go else cp.wait_send()

        @pl.when(jnp.logical_and(along, jnp.logical_and(z >= own, z < Z - 1)))
        def _():
            copy(0, {"tok": me + 4})

        @pl.when(jnp.logical_and(along, jnp.logical_and(z <= own, z > 0)))
        def _():
            copy(1, {"tok": me - 4})

        @pl.when(jnp.logical_and(in_col, jnp.logical_or(jnp.logical_not(both), z == own)))
        def _():
            copy(3, across)

        copy(2, sibling)

    def wait_block(h, w, i):
        rows = pl.ds(pl.multiple_of(i * R, R), R)
        block = wn.at[h, w, rows, :]
        pltpu.make_async_remote_copy(
            block, block, w_send.at[w, i, 2], w_recv.at[h, w, i],
            device_id=sibling, device_id_type=MESH).wait_recv()

    def renew(w):
        def gather(i, _):
            hand_over(w, i).wait_recv()
            return 0

        lax.fori_loop(0, SUM_CHUNKS, gather, 0)

    for w in range(3):

        @pl.when(owns(w))
        def _():
            renew(w)

    is_owner = functools.reduce(jnp.logical_or, [owns(w) for w in range(3)])
    owned_w = jnp.where(owns(0), 0, jnp.where(owns(1), 1, 2))

    @pl.when(is_owner)
    def _():
        wide = m_buf[...].astype(F32)
        norm = jnp.sqrt(jnp.sum(wide * wide)) + 1e-07
        m_buf[...] = (wide / norm).astype(BF16)
        for step in range(NS_STEPS):
            x = m_buf[...]
            g_buf[...] = dot_nt(x, x).astype(BF16)
            g = g_buf[...]
            mixed = (-4.775 * g.astype(F32) + 2.0315 * dot(g, g)).astype(BF16)
            x_buf[...] = 3.4445 * x.astype(F32) + dot(mixed, x)
            m_buf[...] = x_buf[...].astype(BF16)
        for i in range(CHUNKS):
            rows = slice(i * R, (i + 1) * R)
            old = w_ref[owned_w, rows, :].astype(F32)
            fresh = old - m_buf[rows, :].astype(F32)
            scale = jnp.sqrt(
                (jnp.mean(old * old, axis=1, keepdims=True) + 1e-06)
                / (jnp.mean(fresh * fresh, axis=1, keepdims=True) + 1e-06)
            )
            wn[y, owned_w, rows, :] = (fresh * scale).astype(BF16)
            for w in range(3):

                @pl.when(owned_w == w)
                def _():
                    w_copies(w, i, True)

    def spread(t, _):
        for w in range(3):
            h = stream_head(w)
            hops = jnp.abs(z - owner_z(w, h)) + jnp.where(y == h, 0, 1)
            i = t - LAG * (hops - 1) - (WAVE if w == 2 else 0)

            @pl.when(jnp.logical_and(hops > 0, jnp.logical_and(i >= 0, i < CHUNKS)))
            def _():
                wait_block(h, w, i)
                w_copies(w, i, True)

        return 0

    lax.fori_loop(0, CHUNKS + WAVE + LAG * (Z - 1), spread, 0)

    def save(h, w):
        return pltpu.make_async_copy(wn.at[h, w], neww_ref.at[h, w], out_sem.at[h, w])

    def wait_all(h, w):
        def one(i, _):
            wait_block(h, w, i)
            return 0

        lax.fori_loop(0, CHUNKS, one, 0)

    def hidden(h):
        query = q_ref[:, head_cols(h)]
        gate = dot(query, wn[h, 0])
        upper = dot(query, wn[h, 1])
        hid[h] = (gate * jax.nn.sigmoid(gate) * upper).astype(BF16)

    def finish(h):
        out_ref[:, head_cols(h)] = dot(hid[h], wn[h, 2]).astype(BF16)

    loads[4].wait()
    save(c, 0).start()
    save(c, 1).start()
    save(1 - c, 2).start()
    hidden(c)
    wait_all(1 - c, 0)
    save(1 - c, 0).start()
    wait_all(1 - c, 1)
    save(1 - c, 1).start()
    hidden(1 - c)
    finish(1 - c)
    wait_all(c, 2)
    save(c, 2).start()
    finish(c)

    for a in range(2):
        for kind in range(3):
            for j in range(PIECES):
                token_copy(a, j, kind).wait_send()

    def drain_sums(i, _):
        for w in range(3):
            own = owner_z(w, y)

            @pl.when(jnp.logical_not(jnp.logical_and(z == own, c == owner_core(w, y))))
            def _():
                chain_copy(w, i, 1, 0).wait_send()

        return 0

    lax.fori_loop(0, SUM_CHUNKS, drain_sums, 0)

    def drain(i, _):
        for w in range(3):
            w_copies(w, i, False)
        return 0

    lax.fori_loop(0, CHUNKS, drain, 0)
    for h in range(HEADS):
        for w in range(3):
            save(h, w).wait()


def store(a_ref, b_ref, a_out, b_out, sem):
    copies = [
        pltpu.make_async_copy(b_ref, b_out, sem.at[0]),
        pltpu.make_async_copy(a_ref, a_out, sem.at[1]),
    ]
    for cp in copies:
        cp.start()
    for cp in copies:
        cp.wait()


def body(Z, keys, values, queries, rates, fast_weights):
    D = fast_weights.shape[2]
    tokens = keys.shape[0]
    rows = tokens * 4
    sums = D * D // 2 // (SUM_ROWS * SUM_COLS)
    vmem = pl.BlockSpec(memory_space=pltpu.VMEM)
    hbm = pl.BlockSpec(memory_space=pltpu.MemorySpace.HBM)

    def run(*refs):
        kernel(Z, *refs)

    out, fresh = pl.pallas_call(
        run,
        out_shape=(
            jax.ShapeDtypeStruct((tokens, HEADS * D), BF16),
            jax.ShapeDtypeStruct((HEADS, 3, D, D), BF16),
        ),
        in_specs=[hbm] * 5,
        out_specs=(vmem, pl.BlockSpec(memory_space=pl.ANY)),
        scratch_shapes=[
            pltpu.VMEM((tokens, HEADS * D), BF16),
            pltpu.VMEM((tokens, HEADS * D), BF16),
            pltpu.VMEM(rates.shape, F32),
            pltpu.VMEM((3, D, D), BF16),
            pltpu.VMEM((HEADS, tokens, D), BF16),
            pltpu.VMEM((rows, D), BF16),
            pltpu.VMEM((rows, D), BF16),
            pltpu.VMEM((3, rows, D // 2), BF16),
            pltpu.VMEM((2, 3, sums, SUM_ROWS, SUM_COLS), BF16),
            pltpu.VMEM((3, sums, SUM_ROWS, SUM_COLS), BF16),
            pltpu.VMEM((SUM_ROWS, SUM_COLS), F32),
            pltpu.VMEM((D, D), BF16),
            pltpu.VMEM((D, D), F32),
            pltpu.VMEM((D, D), BF16),
            pltpu.VMEM((HEADS, 3, D, D), BF16),
            pltpu.VMEM((HEADS, tokens, D), BF16),
            pltpu.SemaphoreType.DMA((2, 3, PIECES)),
            pltpu.SemaphoreType.DMA((2, 4, PIECES)),
            pltpu.SemaphoreType.DMA((3, sums)),
            pltpu.SemaphoreType.DMA((2, 3, sums)),
            pltpu.SemaphoreType.DMA((sums,)),
            pltpu.SemaphoreType.DMA((3, CHUNKS, 4)),
            pltpu.SemaphoreType.DMA((HEADS, 3, CHUNKS)),
            pltpu.SemaphoreType.DMA((HEADS, 3)),
            pltpu.SemaphoreType.DMA((5,)),
        ],
        compiler_params=pltpu.CompilerParams(
            collective_id=0, has_side_effects=True, vmem_limit_bytes=30 * 1024 * 1024
        ),
        name="ttt_step",
    )(*[pltpu.with_memory_space_constraint(a, pltpu.MemorySpace.HBM) for a in (keys, values, queries, rates, fast_weights)])
    anywhere = pl.BlockSpec(memory_space=pl.ANY)
    return pl.pallas_call(
        store,
        out_shape=(
            jax.ShapeDtypeStruct(out.shape, BF16),
            jax.ShapeDtypeStruct(fresh.shape, BF16),
        ),
        in_specs=[anywhere] * 2,
        out_specs=(hbm, hbm),
        scratch_shapes=[pltpu.SemaphoreType.DMA((2,))],
        compiler_params=pltpu.CompilerParams(vmem_limit_bytes=1024 * 1024),
        name="store",
    )(out, fresh)


def solution(mesh):
    Z = mesh.shape["tok"] // 4
    return jax.shard_map(
        functools.partial(body, Z),
        mesh=mesh,
        in_specs=(
            P(("grp", "tok"), None),
            P(("grp", "tok"), None),
            P(("grp", "tok"), None),
            P(None, ("grp", "tok")),
            P(),
        ),
        out_specs=(P(("grp", "tok"), None), P("grp", None, None, None)),
        check_vma=False,
    )
```

time: 62.1 us -> 61.1 us (0.984)
  Pallas kernels: 61.1 us -> 60.3 us
    pallas_call x1, Pallas kernels: 59.4 us -> 58.6 us  [body(): pl.pallas_call(run, out_shape=(jax.ShapeDtypeStruct((tokens, HEADS * D),...]
where the time goes in v1:
time: 61.1 us; the launch traced here: 61 us
  Pallas kernels  60.3 us (99%)
  between operations  0.64 us (1%)
    pallas_call x1, Pallas kernels, body(): pl.pallas_call(run, out_shape=(jax.ShapeDtypeStruct((tokens, HEADS * D),...  58.6 us
    pallas_call x1, Pallas kernels, body(): pl.pallas_call(store, out_shape=(jax.ShapeDtypeStruct(out.shape, BF16), j...  1.76 us

profile of v1, /device:TPU:0, one launch (start us, length us, event | category | flops | bytes accessed | tf_op | source)
XLA Modules:
  0.0 61.0 jit_solution(971588113679752311)
XLA Ops:
  0.6 58.6 %ttt_step.1 = (bf16[128,1024]{1,0:T(8,128)(2,1)S(1)}, bf16[2,3,512,512]{3,2,1,0:T(8,128)(2,1)S(1)}) custom-call(bf16[128,1024]{1,0:T(8,128)(2,1)} %refs_0_.1, bf16[128,1024]{1,0:T(8,128)(2,1)} %refs_1_.1, bf16[128,1024]{1,0:T(8,128)(2,1)} %refs_2_.1, f32[2,128]{1,0:T(2,128)} %refs_3_.1, bf16[2,3,512,512]{3,2,1,0:T(8,128)(2,1)} %refs_4_.1), custom_call_target="tpu_custom_call" | custom-call | tf_op jit(solution)/shard_map/ttt_step/pallas_call | solution.py:438
  59.2 1.8 %store.1 = (bf16[128,1024]{1,0:T(8,128)(2,1)}, bf16[2,3,512,512]{3,2,1,0:T(8,128)(2,1)}) custom-call(bf16[128,1024]{1,0:T(8,128)(2,1)S(1)} %get-tuple-element.4.a_ref, bf16[2,3,512,512]{3,2,1,0:T(8,128)(2,1)S(1)} %get-tuple-element.5.b_ref), custom_call_target="tpu_custom_call" | custom-call | tf_op jit(solution)/shard_map/store/pallas_call | solution.py:479

commit v2 on v1

v2 whole, which is shorter than its diff:
```python
import functools

import jax
import jax.numpy as jnp
from jax import lax
from jax.experimental import pallas as pl
from jax.experimental.pallas import tpu as pltpu
from jax.sharding import PartitionSpec as P

HEADS = 2
NS_STEPS = 2
CHUNKS = 8
SUM_COLS = 256
SUM_ROWS = 128
SUM_LAG = 6
LAG = 4
WAVE = 4
LEAF = 12
SHIFT = 0
MESH = pl.DeviceIdType.MESH
F32 = jnp.float32
BF16 = jnp.bfloat16


def dot(a, b):
    return jnp.dot(a, b, preferred_element_type=F32)


def dot_nt(a, b):
    return lax.dot_general(a, b, (((1,), (1,)), ((), ())), preferred_element_type=F32)


def dot_tn(a, b):
    return lax.dot_general(a, b, (((0,), (0,)), ((), ())), preferred_element_type=F32)


def kernel(
    Z,
    k_hbm, v_hbm, q_hbm, r_hbm, w_hbm,
    query_ref, neww_ref,
    v_ref, r_ref, w_ref,
    o_loc, keys, outer, gates, grads, recv, sendbuf, part, m_buf, x_buf, g_buf, wn,
    tok_send, tok_recv, chain_send, chain_recv, w_send, w_recv, s_recv, out_sem, in_sem, clear,
):
    tokens = k_hbm.shape[0]
    D = w_ref.shape[1]
    R = D // CHUNKS
    SUM_CHUNKS = D * D // (SUM_ROWS * SUM_COLS)
    me = lax.axis_index("tok")
    c = me % 2
    y = (me // 2) % 2
    z = me // 4

    def mid(h):
        return Z // 2 - 1 + SHIFT * h

    def at(zz, yy, cc):
        return {"tok": (zz * 2 + yy) * 2 + cc}

    def block_rows(p):
        return pl.ds(pl.multiple_of(p * tokens, tokens), tokens)

    def head_cols(h):
        return pl.ds(pl.multiple_of(h * D, D), D)

    sibling = at(z, y, 1 - c)
    across = at(z, 1 - y, c)
    mine = y * 2 + c
    pair = c == y
    gatherer = at(z, 1 - y, 1 - y)

    barrier = pltpu.get_barrier_semaphore()
    for peer in (sibling, across, at(z, 1 - y, 1 - c)):
        pl.semaphore_signal(barrier, inc=1, device_id=peer, device_id_type=MESH)

    @pl.when(z > 0)
    def _():
        pl.semaphore_signal(barrier, inc=1, device_id={"tok": me - 4}, device_id_type=MESH)

    @pl.when(z < Z - 1)
    def _():
        pl.semaphore_signal(barrier, inc=1, device_id={"tok": me + 4}, device_id_type=MESH)

    loads = [
        pltpu.make_async_copy(src, dst, in_sem.at[n])
        for n, (src, dst) in enumerate((
            (r_hbm, r_ref), (v_hbm, v_ref),
            (k_hbm.at[:, head_cols(y)], keys.at[block_rows(mine), :]),
            (w_hbm.at[y], w_ref), (q_hbm, query_ref),
        ))
    ]
    for load in loads:
        load.start()

    loads[0].wait()
    loads[1].wait()
    for h in range(HEADS):
        row = jnp.broadcast_to(r_ref[h : h + 1, :], (128, tokens))
        col = jnp.concatenate([row.T] * (D // 128), axis=1)
        o_loc[h] = (-col * v_ref[:, h * D : (h + 1) * D].astype(F32)).astype(BF16)

    outer[block_rows(mine), :] = o_loc[y]

    pl.semaphore_wait(barrier, 3 + jnp.where(z > 0, 1, 0) + jnp.where(z < Z - 1, 1, 0))

    def token_copy(a, kind):
        h = y if kind == 0 else 1 - y
        src = o_loc.at[h] if a else k_hbm.at[:, head_cols(h)]
        return pltpu.make_async_remote_copy(
            src, (keys, outer)[a].at[block_rows(mine), :],
            tok_send.at[kind], tok_recv.at[a, mine],
            device_id=gatherer if kind else sibling, device_id_type=MESH)

    def pass_on(a, p):
        block = (keys, outer)[a].at[block_rows(p), :]
        return pltpu.make_async_remote_copy(
            block, block, tok_send.at[2], tok_recv.at[a, p],
            device_id=sibling, device_id_type=MESH)

    def token_wait(kind):
        block = keys.at[pl.ds(0, tokens * (4 if kind == 2 else 2)), :]
        return pltpu.make_async_remote_copy(
            block, block, tok_send.at[kind], tok_recv.at[0, 0],
            device_id=sibling, device_id_type=MESH)

    for a in range(2):
        for kind in (1, 0):
            token_copy(a, kind).start()

    loads[2].wait()
    loads[3].wait()

    def forward_step(s, _):
        d = s // 4 * 2 + s % 2
        p = jnp.where(d < 2, y * 2 + jnp.where(d == 0, c, 1 - c), (1 - y) * 2 + d % 2)
        rows = block_rows(p)
        for a in range(2):

            @pl.when(jnp.logical_and(s // 2 % 2 == a, d > 0))
            def _():
                pass_on(a, p).wait_recv()

                @pl.when(jnp.logical_and(pair, d >= 2))
                def _():
                    pass_on(a, p).start()

        @pl.when(s // 2 % 2 == 0)
        def _():
            key = keys[rows, :]
            gate = dot(key, w_ref[0])
            upper = dot(key, w_ref[1])

            @pl.when(pair)
            def _():
                gates[0, rows, :] = gate
                gates[1, rows, :] = upper

            @pl.when(jnp.logical_not(pair))
            def _():
                grads[0, rows, :] = (gate * jax.nn.sigmoid(gate) * upper).astype(BF16)

        @pl.when(jnp.logical_and(pair, s // 2 % 2 == 1))
        def _():
            gate = gates[0, rows, :]
            upper = gates[1, rows, :]
            back = dot_nt(outer[rows, :], w_ref[2])
            sigma = jax.nn.sigmoid(gate)
            grads[0, rows, :] = (back * upper * sigma * (1.0 + gate * (1.0 - sigma))).astype(BF16)
            grads[1, rows, :] = (back * (gate * sigma)).astype(BF16)

        return 0

    lax.fori_loop(0, 8, forward_step, 0)

    def owner_z(w, h):
        return (0, Z - 1, mid(h))[w]

    def slot(w, side=0):
        return w if w < 2 else side

    def chain_copy(w, i, step, side):
        late = jnp.where(i == SUM_CHUNKS - 1, 1, 0)
        return pltpu.make_async_remote_copy(
            sendbuf.at[slot(w), i], recv.at[slot(w, side), i],
            chain_send.at[slot(w), late], chain_recv.at[slot(w, side), i],
            device_id={"tok": me + step * 4}, device_id_type=MESH)

    def chain_sent(w, late):
        block = sendbuf.at[slot(w), pl.ds((SUM_CHUNKS - 1) * late, 1 if late else SUM_CHUNKS - 1)]
        return pltpu.make_async_remote_copy(
            block, block, chain_send.at[slot(w), late], chain_recv.at[slot(w), 0],
            device_id=sibling, device_id_type=MESH)

    def place(i):
        across_cols = D // SUM_COLS
        r = i // across_cols
        q = i % across_cols
        return (
            pl.ds(pl.multiple_of(r * SUM_ROWS, SUM_ROWS), SUM_ROWS),
            pl.ds(pl.multiple_of(q * SUM_COLS, SUM_COLS), SUM_COLS),
        )

    def take(side, w, i):
        chain_copy(w, i, 1, side).wait_recv()
        part[...] += recv[slot(w, side), i].astype(F32)

    def starts(w):
        own = owner_z(w, y)
        return jnp.logical_or(
            jnp.logical_and(z == 0, own != 0), jnp.logical_and(z == Z - 1, own != Z - 1)
        )

    def reduce_event(w, i):
        own = owner_z(w, y)
        rows, cols = place(i)
        if w < 2:
            part[...] = dot_tn(keys[:, rows], grads[w, :, cols])
        else:
            part[...] = dot_tn(grads[0, :, rows], outer[:, cols])

        @pl.when(jnp.logical_and(z > 0, z <= own))
        def _():
            take(0, w, i)

        @pl.when(jnp.logical_and(z < Z - 1, z >= own))
        def _():
            take(1, w, i)

        @pl.when(z == own)
        def _():
            m_buf[rows, cols] = part[...].astype(BF16)

        @pl.when(z != own)
        def _():
            sendbuf[slot(w), i] = part[...].astype(BF16)

        if w == 2:

            @pl.when(jnp.logical_and(starts(w), i == 0))
            def _():
                pl.semaphore_wait(clear, 1)

        @pl.when(z < own)
        def _():
            chain_copy(w, i, 1, 0).start()

        @pl.when(z > own)
        def _():
            chain_copy(w, i, -1, 1).start()

    def depth(w):
        own = owner_z(w, y)
        rise = jnp.where(z <= own, z, 0)
        fall = jnp.where(z >= own, Z - 1 - z, 0)
        return SUM_LAG * jnp.maximum(rise, fall)

    def reduce_step(t, _):
        for w in range(3):
            i = t - depth(w)

            @pl.when(jnp.logical_and(pair == (w < 2), jnp.logical_and(i >= 0, i < SUM_CHUNKS)))
            def _():
                reduce_event(w, i)

        for w in range(2):

            @pl.when(jnp.logical_and(pair, jnp.logical_and(starts(w), t == SUM_CHUNKS - 1)))
            def _():
                chain_sent(w, 0).wait_send()
                pl.semaphore_signal(clear, inc=1, device_id=sibling, device_id_type=MESH)

        return 0

    lax.fori_loop(0, SUM_CHUNKS + SUM_LAG * (Z - 1), reduce_step, 0)

    def stream_head(w):
        return c if w < 2 else 1 - c

    def owns(w):
        h = stream_head(w)
        return jnp.logical_and(y == h, z == owner_z(w, h))

    def w_copies(w, i):
        h = stream_head(w)
        rows = pl.ds(pl.multiple_of(i * R, R), R)
        block = wn.at[h, w, rows, :]

        def copy(kind, dev):
            done = s_recv.at[w] if kind == 2 else w_recv.at[w, i]
            pltpu.make_async_remote_copy(
                block, block, w_send.at[w, kind], done,
                device_id=dev, device_id_type=MESH).start()

        for kind, go, dev in w_targets(w):

            @pl.when(go)
            def _():
                copy(kind, dev)

    def w_targets(w):
        h = stream_head(w)
        own = owner_z(w, h)
        in_col = y == h
        return (
            (0, jnp.logical_and(in_col, jnp.logical_and(z >= own, z < Z - 1)), {"tok": me + 4}),
            (1, jnp.logical_and(in_col, jnp.logical_and(z <= own, z > 0)), {"tok": me - 4}),
            (3, in_col, across),
            (2, z >= 0, sibling),
        )

    def w_wait(h, w, block, send, done):
        return pltpu.make_async_remote_copy(
            block, block, send, done, device_id=sibling, device_id_type=MESH)

    def wait_block(h, w, i):
        rows = pl.ds(pl.multiple_of(i * R, R), R)
        block = wn.at[h, w, rows, :]
        w_wait(h, w, block, w_send.at[w, 2], w_recv.at[w, i]).wait_recv()

    is_owner = functools.reduce(jnp.logical_or, [owns(w) for w in range(3)])
    owned_w = jnp.where(owns(0), 0, jnp.where(owns(1), 1, 2))

    @pl.when(is_owner)
    def _():
        wide = m_buf[...].astype(F32)
        norm = jnp.sqrt(jnp.sum(wide * wide)) + 1e-07
        m_buf[...] = (wide / norm).astype(BF16)
        for step in range(NS_STEPS):
            x = m_buf[...]
            g_buf[...] = dot_nt(x, x).astype(BF16)
            g = g_buf[...]
            mixed = (-4.775 * g.astype(F32) + 2.0315 * dot(g, g)).astype(BF16)
            x_buf[...] = 3.4445 * x.astype(F32) + dot(mixed, x)
            m_buf[...] = x_buf[...].astype(BF16)
        for i in range(CHUNKS):
            rows = slice(i * R, (i + 1) * R)
            old = w_ref[owned_w, rows, :].astype(F32)
            fresh = old - m_buf[rows, :].astype(F32)
            scale = jnp.sqrt(
                (jnp.mean(old * old, axis=1, keepdims=True) + 1e-06)
                / (jnp.mean(fresh * fresh, axis=1, keepdims=True) + 1e-06)
            )
            wn[y, owned_w, rows, :] = (fresh * scale).astype(BF16)
            for w in range(3):

                @pl.when(owned_w == w)
                def _():
                    w_copies(w, i)

    def spread(t, _):
        for w in range(3):
            h = stream_head(w)
            own = owner_z(w, h)
            hops = jnp.abs(z - own) + jnp.where(y == h, 0, 1)
            shared = (jnp.logical_and(z > mid(h), w == 0), jnp.logical_and(z < mid(h), w == 1), False)[w]
            stride = jnp.where(shared, 2, 1)
            u = t - LAG * (hops - 1) - (WAVE if w == 2 else 0) - jnp.where(y == h, 0, LEAF)
            i = jnp.where(shared, (u + 16) // 2 - 8, u)

            @pl.when(jnp.logical_and(
                jnp.logical_and(hops > 0, jnp.logical_or(jnp.logical_not(shared), u % 2 == 0)),
                jnp.logical_and(u >= 0, i < CHUNKS)))
            def _():
                wait_block(h, w, i)
                w_copies(w, i)

        return 0

    lax.fori_loop(0, 2 * CHUNKS + WAVE + LEAF + LAG * (Z - 1), spread, 0)

    def save(h, w):
        return pltpu.make_async_copy(wn.at[h, w], neww_ref.at[h, w], out_sem.at[0])

    def finish(w):
        h = 1 - stream_head(w)
        w_wait(h, w, wn.at[h, w], w_send.at[w, 2], s_recv.at[w]).wait_recv()
        save(h, w).start()

    for w in range(3):
        save(stream_head(w), w).start()
    for w in range(3):
        finish(w)
    loads[4].wait()

    for kind in range(2):
        token_wait(kind).wait_send()

    @pl.when(pair)
    def _():
        token_wait(2).wait_send()

    for w in range(3):
        moved = jnp.logical_and(pair == (w < 2), z != owner_z(w, y))

        @pl.when(jnp.logical_and(moved, jnp.logical_not(starts(w))) if w < 2 else moved)
        def _():
            chain_sent(w, 0).wait_send()

        @pl.when(moved)
        def _():
            chain_sent(w, 1).wait_send()

        for kind, go, _ in w_targets(w):

            @pl.when(go)
            def _():
                w_wait(0, w, wn.at[stream_head(w), w], w_send.at[w, kind], s_recv.at[w]).wait_send()

    pltpu.make_async_copy(wn, neww_ref, out_sem.at[0]).wait()


def readout(query_ref, w_ref, out, w_out, out_v, sem):
    copies = [
        pltpu.make_async_copy(w_ref, w_out, sem.at[0]),
        pltpu.make_async_copy(out_v, out, sem.at[1]),
    ]
    copies[0].start()
    D = w_ref.shape[2]
    for h in range(HEADS):
        cols = slice(h * D, (h + 1) * D)
        query = query_ref[:, cols]
        gate = dot(query, w_ref[h, 0])
        upper = dot(query, w_ref[h, 1])
        hidden = (gate * jax.nn.sigmoid(gate) * upper).astype(BF16)
        out_v[:, cols] = dot(hidden, w_ref[h, 2]).astype(BF16)
    copies[1].start()
    for cp in copies:
        cp.wait()


def body(Z, keys, values, queries, rates, fast_weights):
    D = fast_weights.shape[2]
    tokens = keys.shape[0]
    rows = tokens * 4
    sums = D * D // (SUM_ROWS * SUM_COLS)
    vmem = pl.BlockSpec(memory_space=pltpu.VMEM)
    hbm = pl.BlockSpec(memory_space=pltpu.MemorySpace.HBM)

    def run(*refs):
        kernel(Z, *refs)

    query, fresh = pl.pallas_call(
        run,
        out_shape=(
            jax.ShapeDtypeStruct((tokens, HEADS * D), BF16),
            jax.ShapeDtypeStruct((HEADS, 3, D, D), BF16),
        ),
        in_specs=[hbm] * 5,
        out_specs=(pl.BlockSpec(memory_space=pl.ANY), pl.BlockSpec(memory_space=pl.ANY)),
        scratch_shapes=[
            pltpu.VMEM((tokens, HEADS * D), BF16),
            pltpu.VMEM(rates.shape, F32),
            pltpu.VMEM((3, D, D), BF16),
            pltpu.VMEM((HEADS, tokens, D), BF16),
            pltpu.VMEM((rows, D), BF16),
            pltpu.VMEM((rows, D), BF16),
            pltpu.VMEM((2, rows, D), F32),
            pltpu.VMEM((2, rows, D), BF16),
            pltpu.VMEM((2, sums, SUM_ROWS, SUM_COLS), BF16),
            pltpu.VMEM((2, sums, SUM_ROWS, SUM_COLS), BF16),
            pltpu.VMEM((SUM_ROWS, SUM_COLS), F32),
            pltpu.VMEM((D, D), BF16),
            pltpu.VMEM((D, D), F32),
            pltpu.VMEM((D, D), BF16),
            pltpu.VMEM((HEADS, 3, D, D), BF16),
            pltpu.SemaphoreType.DMA((3,)),
            pltpu.SemaphoreType.DMA((2, 4)),
            pltpu.SemaphoreType.DMA((2, 2)),
            pltpu.SemaphoreType.DMA((2, sums)),
            pltpu.SemaphoreType.DMA((3, 4)),
            pltpu.SemaphoreType.DMA((3, CHUNKS)),
            pltpu.SemaphoreType.DMA((3,)),
            pltpu.SemaphoreType.DMA((1,)),
            pltpu.SemaphoreType.DMA((5,)),
            pltpu.SemaphoreType.REGULAR,
        ],
        compiler_params=pltpu.CompilerParams(
            collective_id=0, has_side_effects=True, vmem_limit_bytes=30 * 1024 * 1024
        ),
        name="ttt_step",
    )(*[pltpu.with_memory_space_constraint(a, pltpu.MemorySpace.HBM) for a in (keys, values, queries, rates, fast_weights)])
    return pl.pallas_call(
        readout,
        out_shape=(
            jax.ShapeDtypeStruct(query.shape, BF16),
            jax.ShapeDtypeStruct(fresh.shape, BF16),
        ),
        in_specs=[vmem] * 2,
        out_specs=(hbm, hbm),
        scratch_shapes=[
            pltpu.VMEM(query.shape, BF16),
            pltpu.SemaphoreType.DMA((2,)),
        ],
        compiler_params=pltpu.CompilerParams(vmem_limit_bytes=4 * 1024 * 1024),
        name="readout",
    )(query, fresh)


def solution(mesh):
    Z = mesh.shape["tok"] // 4
    return jax.shard_map(
        functools.partial(body, Z),
        mesh=mesh,
        in_specs=(
            P(("grp", "tok"), None),
            P(("grp", "tok"), None),
            P(("grp", "tok"), None),
            P(None, ("grp", "tok")),
            P(),
        ),
        out_specs=(P(("grp", "tok"), None), P("grp", None, None, None)),
        check_vma=False,
    )
```

time: 61.1 us -> 56.3 us (0.921)
  the two profiles are of different devices: /device:TPU:0 before, /device:TPU:21 now
where the time goes in v2:
time: 56.3 us; the launch traced here: 56.2 us
  Pallas kernels  55.5 us (99%)
  between operations  0.64 us (1%)
    pallas_call x1, Pallas kernels, body(): pl.pallas_call(run, out_shape=(jax.ShapeDtypeStruct((tokens, HEADS * D),...  53.8 us
    pallas_call x1, Pallas kernels, body(): pl.pallas_call(readout, out_shape=(jax.ShapeDtypeStruct(query.shape, BF16...  1.77 us

profile of v2, /device:TPU:21, one launch (start us, length us, event | category | flops | bytes accessed | tf_op | source)
XLA Modules:
  0.0 56.2 jit_solution(6702688551204655847)
XLA Ops:
  0.6 53.8 %ttt_step.1 = (bf16[128,1024]{1,0:T(8,128)(2,1)S(1)}, bf16[2,3,512,512]{3,2,1,0:T(8,128)(2,1)S(1)}) custom-call(bf16[128,1024]{1,0:T(8,128)(2,1)} %refs_0_.1, bf16[128,1024]{1,0:T(8,128)(2,1)} %refs_1_.1, bf16[128,1024]{1,0:T(8,128)(2,1)} %refs_2_.1, f32[2,128]{1,0:T(2,128)} %refs_3_.1, bf16[2,3,512,512]{3,2,1,0:T(8,128)(2,1)} %refs_4_.1), custom_call_target="tpu_custom_call" | custom-call | tf_op jit(solution)/shard_map/ttt_step/pallas_call | solution.py:442
  54.4 1.8 %readout.1 = (bf16[128,1024]{1,0:T(8,128)(2,1)}, bf16[2,3,512,512]{3,2,1,0:T(8,128)(2,1)}) custom-call(bf16[128,1024]{1,0:T(8,128)(2,1)S(1)} %get-tuple-element.4.query_ref, bf16[2,3,512,512]{3,2,1,0:T(8,128)(2,1)S(1)} %get-tuple-element.5.w_ref), custom_call_target="tpu_custom_call" | custom-call | tf_op jit(solution)/shard_map/readout/pallas_call | solution.py:482

commit v3 on v2

--- a/solution.py
+++ b/solution.py
@@ -12,9 +12,8 @@
 CHUNKS = 8
 SUM_COLS = 256
 SUM_ROWS = 128
-SUM_LAG = 6
+SUM_LAG = 4
 LAG = 4
-WAVE = 4
 LEAF = 12
 SHIFT = 0
 MESH = pl.DeviceIdType.MESH
@@ -66,8 +65,8 @@
     sibling = at(z, y, 1 - c)
     across = at(z, 1 - y, c)
     mine = y * 2 + c
-    pair = c == y
-    gatherer = at(z, 1 - y, 1 - y)
+    pair = c == 1
+    gatherer = at(z, 1 - y, 1)
 
     barrier = pltpu.get_barrier_semaphore()
     for peer in (sibling, across, at(z, 1 - y, 1 - c)):
@@ -254,68 +253,89 @@
         fall = jnp.where(z >= own, Z - 1 - z, 0)
         return SUM_LAG * jnp.maximum(rise, fall)
 
-    def reduce_step(t, _):
-        for w in range(3):
-            i = t - depth(w)
-
-            @pl.when(jnp.logical_and(pair == (w < 2), jnp.logical_and(i >= 0, i < SUM_CHUNKS)))
-            def _():
-                reduce_event(w, i)
-
-        for w in range(2):
-
-            @pl.when(jnp.logical_and(pair, jnp.logical_and(starts(w), t == SUM_CHUNKS - 1)))
-            def _():
-                chain_sent(w, 0).wait_send()
-                pl.semaphore_signal(clear, inc=1, device_id=sibling, device_id_type=MESH)
-
-        return 0
-
-    lax.fori_loop(0, SUM_CHUNKS + SUM_LAG * (Z - 1), reduce_step, 0)
-
-    def stream_head(w):
-        return c if w < 2 else 1 - c
+    def reduce_all(ws):
+        depths = [depth(w) for w in ws]
+        first = [starts(w) for w in ws]
+
+        def step(t, _):
+            for w, lag in zip(ws, depths):
+                i = t - lag
+
+                @pl.when(jnp.logical_and(i >= 0, i < SUM_CHUNKS))
+                def _():
+                    reduce_event(w, i)
+
+            if len(ws) == 2:
+                for w, head in zip(ws, first):
+
+                    @pl.when(jnp.logical_and(head, t == SUM_CHUNKS - 1))
+                    def _():
+                        chain_sent(w, 0).wait_send()
+                        pl.semaphore_signal(clear, inc=1, device_id=sibling, device_id_type=MESH)
+
+            return 0
+
+        lax.fori_loop(0, SUM_CHUNKS + functools.reduce(jnp.maximum, depths), step, 0)
+
+    @pl.when(pair)
+    def _():
+        reduce_all((0, 1))
+
+    @pl.when(jnp.logical_not(pair))
+    def _():
+        reduce_all((2,))
 
     def owns(w):
-        h = stream_head(w)
-        return jnp.logical_and(y == h, z == owner_z(w, h))
-
-    def w_copies(w, i):
-        h = stream_head(w)
+        return jnp.logical_and(pair == (w < 2), z == owner_z(w, y))
+
+    def stream(h, w):
+        return h * 2 + w % 2
+
+    def w_targets(w, home):
+        own = owner_z(w, y)
+        leaf = (2, True, sibling)
+        if not home:
+            return (leaf,)
+        return (
+            (0, jnp.logical_and(z >= own, z < Z - 1), {"tok": me + 4}),
+            (1, jnp.logical_and(z <= own, z > 0), {"tok": me - 4}),
+            (3, True, across),
+            leaf,
+        )
+
+    def w_copies(h, w, i, targets):
         rows = pl.ds(pl.multiple_of(i * R, R), R)
         block = wn.at[h, w, rows, :]
+        n = stream(h, w)
 
         def copy(kind, dev):
-            done = s_recv.at[w] if kind == 2 else w_recv.at[w, i]
             pltpu.make_async_remote_copy(
-                block, block, w_send.at[w, kind], done,
+                block, block, w_send.at[n, kind], s_recv.at[n] if kind == 2 else w_recv.at[n, i],
                 device_id=dev, device_id_type=MESH).start()
 
-        for kind, go, dev in w_targets(w):
-
-            @pl.when(go)
-            def _():
+        for kind, go, dev in targets:
+            if go is True:
                 copy(kind, dev)
-
-    def w_targets(w):
-        h = stream_head(w)
-        own = owner_z(w, h)
-        in_col = y == h
-        return (
-            (0, jnp.logical_and(in_col, jnp.logical_and(z >= own, z < Z - 1)), {"tok": me + 4}),
-            (1, jnp.logical_and(in_col, jnp.logical_and(z <= own, z > 0)), {"tok": me - 4}),
-            (3, in_col, across),
-            (2, z >= 0, sibling),
-        )
-
-    def w_wait(h, w, block, send, done):
+            else:
+
+                @pl.when(go)
+                def _():
+                    copy(kind, dev)
+
+    def w_wait(h, w, kind):
+        block = wn.at[h, w]
+        n = stream(h, w)
         return pltpu.make_async_remote_copy(
-            block, block, send, done, device_id=sibling, device_id_type=MESH)
+            block, block, w_send.at[n, kind], s_recv.at[n],
+            device_id=sibling, device_id_type=MESH)
 
     def wait_block(h, w, i):
         rows = pl.ds(pl.multiple_of(i * R, R), R)
         block = wn.at[h, w, rows, :]
-        w_wait(h, w, block, w_send.at[w, 2], w_recv.at[w, i]).wait_recv()
+        n = stream(h, w)
+        pltpu.make_async_remote_copy(
+            block, block, w_send.at[n, 2], w_recv.at[n, i],
+            device_id=sibling, device_id_type=MESH).wait_recv()
 
     is_owner = functools.reduce(jnp.logical_or, [owns(w) for w in range(3)])
     owned_w = jnp.where(owns(0), 0, jnp.where(owns(1), 1, 2))
@@ -332,6 +352,10 @@
             mixed = (-4.775 * g.astype(F32) + 2.0315 * dot(g, g)).astype(BF16)
             x_buf[...] = 3.4445 * x.astype(F32) + dot(mixed, x)
             m_buf[...] = x_buf[...].astype(BF16)
+        edges = (
+            (0, z < Z - 1, {"tok": me + 4}), (1, z > 0, {"tok": me - 4}),
+            (3, True, across), (2, True, sibling),
+        )
         for i in range(CHUNKS):
             rows = slice(i * R, (i + 1) * R)
             old = w_ref[owned_w, rows, :].astype(F32)
@@ -341,45 +365,53 @@
                 / (jnp.mean(fresh * fresh, axis=1, keepdims=True) + 1e-06)
             )
             wn[y, owned_w, rows, :] = (fresh * scale).astype(BF16)
-            for w in range(3):
-
-                @pl.when(owned_w == w)
+            w_copies(y, owned_w, i, edges)
+
+    def spread_all(ws):
+        routes = []
+        end = 0
+        for home in (True, False):
+            h = y if home else 1 - y
+            for w in ws:
+                hops = jnp.abs(z - owner_z(w, h)) + (0 if home else 1)
+                start = LAG * (hops - 1) + (0 if home else LEAF)
+                routes.append((h, w, start, hops > 0, w_targets(w, home)))
+                end = jnp.maximum(end, start + CHUNKS)
+
+        def step(t, _):
+            for h, w, start, live, targets in routes:
+                i = t - start
+
+                @pl.when(jnp.logical_and(live, jnp.logical_and(i >= 0, i < CHUNKS)))
                 def _():
-                    w_copies(w, i)
-
-    def spread(t, _):
-        for w in range(3):
-            h = stream_head(w)
-            own = owner_z(w, h)
-            hops = jnp.abs(z - own) + jnp.where(y == h, 0, 1)
-            shared = (jnp.logical_and(z > mid(h), w == 0), jnp.logical_and(z < mid(h), w == 1), False)[w]
-            stride = jnp.where(shared, 2, 1)
-            u = t - LAG * (hops - 1) - (WAVE if w == 2 else 0) - jnp.where(y == h, 0, LEAF)
-            i = jnp.where(shared, (u + 16) // 2 - 8, u)
-
-            @pl.when(jnp.logical_and(
-                jnp.logical_and(hops > 0, jnp.logical_or(jnp.logical_not(shared), u % 2 == 0)),
-                jnp.logical_and(u >= 0, i < CHUNKS)))
-            def _():
-                wait_block(h, w, i)
-                w_copies(w, i)
-
-        return 0
-
-    lax.fori_loop(0, 2 * CHUNKS + WAVE + LEAF + LAG * (Z - 1), spread, 0)
+                    wait_block(h, w, i)
+                    w_copies(h, w, i, targets)
+
+            return 0
+
+        lax.fori_loop(0, end, step, 0)
+
+    @pl.when(pair)
+    def _():
+        spread_all((0, 1))
+
+    @pl.when(jnp.logical_not(pair))
+    def _():
+        spread_all((2,))
 
     def save(h, w):
         return pltpu.make_async_copy(wn.at[h, w], neww_ref.at[h, w], out_sem.at[0])
 
-    def finish(w):
-        h = 1 - stream_head(w)
-        w_wait(h, w, wn.at[h, w], w_send.at[w, 2], s_recv.at[w]).wait_recv()
-        save(h, w).start()
-
-    for w in range(3):
-        save(stream_head(w), w).start()
-    for w in range(3):
-        finish(w)
+    for mine_first in (True, False):
+        for w in range(3):
+
+            @pl.when((pair == (w < 2)) == mine_first)
+            def _():
+                for h in range(HEADS):
+                    if not mine_first:
+                        w_wait(h, w, 2).wait_recv()
+                    save(h, w).start()
+
     loads[4].wait()
 
     for kind in range(2):
@@ -400,11 +432,15 @@
         def _():
             chain_sent(w, 1).wait_send()
 
-        for kind, go, _ in w_targets(w):
-
-            @pl.when(go)
-            def _():
-                w_wait(0, w, wn.at[stream_head(w), w], w_send.at[w, kind], s_recv.at[w]).wait_send()
+        @pl.when(pair == (w < 2))
+        def _():
+            for home in (True, False):
+                h = y if home else 1 - y
+                for kind, go, _ in w_targets(w, home):
+
+                    @pl.when(go)
+                    def _():
+                        w_wait(h, w, kind).wait_send()
 
     pltpu.make_async_copy(wn, neww_ref, out_sem.at[0]).wait()
 
@@ -467,9 +503,9 @@
             pltpu.SemaphoreType.DMA((2, 4)),
             pltpu.SemaphoreType.DMA((2, 2)),
             pltpu.SemaphoreType.DMA((2, sums)),
-            pltpu.SemaphoreType.DMA((3, 4)),
-            pltpu.SemaphoreType.DMA((3, CHUNKS)),
-            pltpu.SemaphoreType.DMA((3,)),
+            pltpu.SemaphoreType.DMA((4, 4)),
+            pltpu.SemaphoreType.DMA((4, CHUNKS)),
+            pltpu.SemaphoreType.DMA((4,)),
             pltpu.SemaphoreType.DMA((1,)),
             pltpu.SemaphoreType.DMA((5,)),
             pltpu.SemaphoreType.REGULAR,

time: 56.3 us -> 54.3 us (0.964)
  the two profiles are of different devices: /device:TPU:21 before, /device:TPU:0 now
where the time goes in v3:
time: 54.3 us; the launch traced here: 54.2 us
  Pallas kernels  53.5 us (99%)
  between operations  0.64 us (1%)
    pallas_call x1, Pallas kernels, body(): pl.pallas_call(run, out_shape=(jax.ShapeDtypeStruct((tokens, HEADS * D),...  51.8 us
    pallas_call x1, Pallas kernels, body(): pl.pallas_call(readout, out_shape=(jax.ShapeDtypeStruct(query.shape, BF16...  1.77 us

profile of v3, /device:TPU:0, one launch (start us, length us, event | category | flops | bytes accessed | tf_op | source)
XLA Modules:
  0.0 54.2 jit_solution(2818507195405091215)
XLA Ops:
  0.6 51.8 %ttt_step.1 = (bf16[128,1024]{1,0:T(8,128)(2,1)S(1)}, bf16[2,3,512,512]{3,2,1,0:T(8,128)(2,1)S(1)}) custom-call(bf16[128,1024]{1,0:T(8,128)(2,1)} %refs_0_.1, bf16[128,1024]{1,0:T(8,128)(2,1)} %refs_1_.1, bf16[128,1024]{1,0:T(8,128)(2,1)} %refs_2_.1, f32[2,128]{1,0:T(2,128)} %refs_3_.1, bf16[2,3,512,512]{3,2,1,0:T(8,128)(2,1)} %refs_4_.1), custom_call_target="tpu_custom_call" | custom-call | tf_op jit(solution)/shard_map/ttt_step/pallas_call | solution.py:478
  52.4 1.8 %readout.1 = (bf16[128,1024]{1,0:T(8,128)(2,1)}, bf16[2,3,512,512]{3,2,1,0:T(8,128)(2,1)}) custom-call(bf16[128,1024]{1,0:T(8,128)(2,1)S(1)} %get-tuple-element.4.query_ref, bf16[2,3,512,512]{3,2,1,0:T(8,128)(2,1)S(1)} %get-tuple-element.5.w_ref), custom_call_target="tpu_custom_call" | custom-call | tf_op jit(solution)/shard_map/readout/pallas_call | solution.py:518

commit v4 on v3

--- a/solution.py
+++ b/solution.py
@@ -9,12 +9,11 @@
 
 HEADS = 2
 NS_STEPS = 2
-CHUNKS = 8
-SUM_COLS = 256
-SUM_ROWS = 128
-SUM_LAG = 4
-LAG = 4
-LEAF = 12
+CHUNKS = 16
+SUM_CHUNKS = 16
+SUM_LAG = 7
+LAG = 6
+LEAF = 16
 SHIFT = 0
 MESH = pl.DeviceIdType.MESH
 F32 = jnp.float32
@@ -38,13 +37,13 @@
     k_hbm, v_hbm, q_hbm, r_hbm, w_hbm,
     query_ref, neww_ref,
     v_ref, r_ref, w_ref,
-    o_loc, keys, outer, gates, grads, recv, sendbuf, part, m_buf, x_buf, g_buf, wn,
-    tok_send, tok_recv, chain_send, chain_recv, w_send, w_recv, s_recv, out_sem, in_sem, clear,
+    o_loc, keys, outer, gates, grads, sums, recv, sendbuf, square, m_buf, x_buf, g_buf, wn,
+    tok_send, tok_recv, chain_send, chain_recv, w_send, w_recv, s_recv, out_sem, in_sem,
 ):
     tokens = k_hbm.shape[0]
     D = w_ref.shape[1]
     R = D // CHUNKS
-    SUM_CHUNKS = D * D // (SUM_ROWS * SUM_COLS)
+    S = D // SUM_CHUNKS
     me = lax.axis_index("tok")
     c = me % 2
     y = (me // 2) % 2
@@ -67,6 +66,8 @@
     mine = y * 2 + c
     pair = c == 1
     gatherer = at(z, 1 - y, 1)
+    middle = z == mid(y)
+    sums_here = jnp.logical_or(pair, middle)
 
     barrier = pltpu.get_barrier_semaphore()
     for peer in (sibling, across, at(z, 1 - y, 1 - c)):
@@ -90,17 +91,7 @@
     ]
     for load in loads:
         load.start()
-
-    loads[0].wait()
-    loads[1].wait()
-    for h in range(HEADS):
-        row = jnp.broadcast_to(r_ref[h : h + 1, :], (128, tokens))
-        col = jnp.concatenate([row.T] * (D // 128), axis=1)
-        o_loc[h] = (-col * v_ref[:, h * D : (h + 1) * D].astype(F32)).astype(BF16)
-
-    outer[block_rows(mine), :] = o_loc[y]
-
-    pl.semaphore_wait(barrier, 3 + jnp.where(z > 0, 1, 0) + jnp.where(z < Z - 1, 1, 0))
+    square[...] = jnp.zeros_like(square)
 
     def token_copy(a, kind):
         h = y if kind == 0 else 1 - y
@@ -122,10 +113,24 @@
             block, block, tok_send.at[kind], tok_recv.at[0, 0],
             device_id=sibling, device_id_type=MESH)
 
-    for a in range(2):
-        for kind in (1, 0):
-            token_copy(a, kind).start()
-
+    def send_tokens(a):
+        token_copy(a, 1).start()
+
+        @pl.when(jnp.logical_or(jnp.logical_not(pair), middle))
+        def _():
+            token_copy(a, 0).start()
+
+    pl.semaphore_wait(barrier, 3 + jnp.where(z > 0, 1, 0) + jnp.where(z < Z - 1, 1, 0))
+    send_tokens(0)
+    loads[0].wait()
+    loads[1].wait()
+    for h in range(HEADS):
+        row = jnp.broadcast_to(r_ref[h : h + 1, :], (128, tokens))
+        col = jnp.concatenate([row.T] * (D // 128), axis=1)
+        o_loc[h] = (-col * v_ref[:, h * D : (h + 1) * D].astype(F32)).astype(BF16)
+
+    send_tokens(1)
+    outer[block_rows(mine), :] = o_loc[y]
     loads[2].wait()
     loads[3].wait()
 
@@ -139,7 +144,7 @@
             def _():
                 pass_on(a, p).wait_recv()
 
-                @pl.when(jnp.logical_and(pair, d >= 2))
+                @pl.when(jnp.logical_and(jnp.logical_and(pair, middle), d >= 2))
                 def _():
                     pass_on(a, p).start()
 
@@ -149,14 +154,9 @@
             gate = dot(key, w_ref[0])
             upper = dot(key, w_ref[1])
 
-            @pl.when(pair)
-            def _():
-                gates[0, rows, :] = gate
-                gates[1, rows, :] = upper
-
-            @pl.when(jnp.logical_not(pair))
-            def _():
-                grads[0, rows, :] = (gate * jax.nn.sigmoid(gate) * upper).astype(BF16)
+            gates[0, rows, :] = gate
+            gates[1, rows, :] = upper
+            grads[2, rows, :] = (gate * jax.nn.sigmoid(gate) * upper).astype(BF16)
 
         @pl.when(jnp.logical_and(pair, s // 2 % 2 == 1))
         def _():
@@ -169,81 +169,67 @@
 
         return 0
 
-    lax.fori_loop(0, 8, forward_step, 0)
+    lax.fori_loop(0, jnp.where(sums_here, 8, 0), forward_step, 0)
 
     def owner_z(w, h):
         return (0, Z - 1, mid(h))[w]
 
-    def slot(w, side=0):
-        return w if w < 2 else side
-
     def chain_copy(w, i, step, side):
-        late = jnp.where(i == SUM_CHUNKS - 1, 1, 0)
+        there = z + step == mid(y)
+        held = jnp.where(there, side, 2) if w == 2 else w
+        core = jnp.where(there, 0, 1) if w == 2 else 1
         return pltpu.make_async_remote_copy(
-            sendbuf.at[slot(w), i], recv.at[slot(w, side), i],
-            chain_send.at[slot(w), late], chain_recv.at[slot(w, side), i],
-            device_id={"tok": me + step * 4}, device_id_type=MESH)
-
-    def chain_sent(w, late):
-        block = sendbuf.at[slot(w), pl.ds((SUM_CHUNKS - 1) * late, 1 if late else SUM_CHUNKS - 1)]
+            sendbuf.at[w, i], recv.at[held, i], chain_send.at[w], chain_recv.at[held, i],
+            device_id=at(z + step, y, core), device_id_type=MESH)
+
+    def chain_sent(w):
+        block = sendbuf.at[w]
         return pltpu.make_async_remote_copy(
-            block, block, chain_send.at[slot(w), late], chain_recv.at[slot(w), 0],
+            block, block, chain_send.at[w], chain_recv.at[w, 0],
             device_id=sibling, device_id_type=MESH)
 
-    def place(i):
-        across_cols = D // SUM_COLS
-        r = i // across_cols
-        q = i % across_cols
+    def chain_roles(w):
+        own = owner_z(w, y)
         return (
-            pl.ds(pl.multiple_of(r * SUM_ROWS, SUM_ROWS), SUM_ROWS),
-            pl.ds(pl.multiple_of(q * SUM_COLS, SUM_COLS), SUM_COLS),
+            jnp.logical_and(z > 0, z <= own), jnp.logical_and(z < Z - 1, z >= own),
+            z == own, z < own, z > own,
         )
 
-    def take(side, w, i):
-        chain_copy(w, i, 1, side).wait_recv()
-        part[...] += recv[slot(w, side), i].astype(F32)
-
-    def starts(w):
-        own = owner_z(w, y)
-        return jnp.logical_or(
-            jnp.logical_and(z == 0, own != 0), jnp.logical_and(z == Z - 1, own != Z - 1)
-        )
-
-    def reduce_event(w, i):
-        own = owner_z(w, y)
-        rows, cols = place(i)
-        if w < 2:
-            part[...] = dot_tn(keys[:, rows], grads[w, :, cols])
-        else:
-            part[...] = dot_tn(grads[0, :, rows], outer[:, cols])
-
-        @pl.when(jnp.logical_and(z > 0, z <= own))
-        def _():
-            take(0, w, i)
-
-        @pl.when(jnp.logical_and(z < Z - 1, z >= own))
-        def _():
-            take(1, w, i)
-
-        @pl.when(z == own)
-        def _():
-            m_buf[rows, cols] = part[...].astype(BF16)
-
-        @pl.when(z != own)
-        def _():
-            sendbuf[slot(w), i] = part[...].astype(BF16)
-
-        if w == 2:
-
-            @pl.when(jnp.logical_and(starts(w), i == 0))
-            def _():
-                pl.semaphore_wait(clear, 1)
-
-        @pl.when(z < own)
+    def reduce_event(w, i, roles):
+        below, above, ends, rises, falls = roles
+        rows = pl.ds(pl.multiple_of(i * S, S), S)
+
+        def take(side):
+            held = jnp.where(middle, side, 2) if w == 2 else w
+            block = recv.at[held, i]
+            pltpu.make_async_remote_copy(
+                block, block, chain_send.at[w], chain_recv.at[held, i],
+                device_id=sibling, device_id_type=MESH).wait_recv()
+            sums[w, rows, :] += recv[held, i].astype(F32)
+
+        @pl.when(below)
+        def _():
+            take(0)
+
+        @pl.when(above)
+        def _():
+            take(1)
+
+        @pl.when(ends)
+        def _():
+            rounded = sums[w, rows, :].astype(BF16)
+            m_buf[rows, :] = rounded
+            square[...] += jnp.square(rounded.astype(F32))
+
+        @pl.when(jnp.logical_not(ends))
+        def _():
+            sendbuf[w, i] = sums[w, rows, :].astype(BF16)
+
+        @pl.when(rises)
         def _():
             chain_copy(w, i, 1, 0).start()
 
-        @pl.when(z > own)
+        @pl.when(falls)
         def _():
             chain_copy(w, i, -1, 1).start()
 
@@ -253,37 +239,44 @@
         fall = jnp.where(z >= own, Z - 1 - z, 0)
         return SUM_LAG * jnp.maximum(rise, fall)
 
-    def reduce_all(ws):
-        depths = [depth(w) for w in ws]
-        first = [starts(w) for w in ws]
+    def reduce_all(ws, depths, live):
+        roles = [chain_roles(w) for w in ws]
 
         def step(t, _):
-            for w, lag in zip(ws, depths):
+            for w, lag, role, on in zip(ws, depths, roles, live):
                 i = t - lag
 
-                @pl.when(jnp.logical_and(i >= 0, i < SUM_CHUNKS))
+                @pl.when(jnp.logical_and(on, jnp.logical_and(i >= 0, i < SUM_CHUNKS)))
                 def _():
-                    reduce_event(w, i)
-
-            if len(ws) == 2:
-                for w, head in zip(ws, first):
-
-                    @pl.when(jnp.logical_and(head, t == SUM_CHUNKS - 1))
-                    def _():
-                        chain_sent(w, 0).wait_send()
-                        pl.semaphore_signal(clear, inc=1, device_id=sibling, device_id_type=MESH)
+                    reduce_event(w, i, role)
 
             return 0
 
-        lax.fori_loop(0, SUM_CHUNKS + functools.reduce(jnp.maximum, depths), step, 0)
+        return step
 
     @pl.when(pair)
     def _():
-        reduce_all((0, 1))
-
-    @pl.when(jnp.logical_not(pair))
-    def _():
-        reduce_all((2,))
+        depths = [depth(0), depth(1), depth(2) + SUM_CHUNKS]
+        step = reduce_all((0, 1, 2), depths, (True, True, jnp.logical_not(middle)))
+        near = jnp.where(2 * z < Z, 1, 0)
+        edge = jnp.logical_or(z == 0, z == Z - 1)
+        first = jnp.where(edge, SUM_CHUNKS, 0)
+
+        def near_part(n, _):
+            rows = pl.ds(pl.multiple_of(n * (D // 4), D // 4), D // 4)
+            sums[near, rows, :] = dot_tn(keys[:, rows], grads[near])
+            lax.fori_loop(first * n // 4, first * (n + 1) // 4, step, 0)
+            return 0
+
+        lax.fori_loop(0, 4, near_part, 0)
+        sums[1 - near] = dot_tn(keys[...], grads[1 - near])
+        sums[2] = dot_tn(grads[2], outer[...])
+        lax.fori_loop(first, SUM_CHUNKS + functools.reduce(jnp.maximum, depths), step, 0)
+
+    @pl.when(jnp.logical_and(jnp.logical_not(pair), middle))
+    def _():
+        sums[2] = dot_tn(grads[2], outer[...])
+        lax.fori_loop(0, SUM_CHUNKS, reduce_all((2,), (0,), (True,)), 0)
 
     def owns(w):
         return jnp.logical_and(pair == (w < 2), z == owner_z(w, y))
@@ -303,6 +296,9 @@
             leaf,
         )
 
+    def arrival(w, leaf, i):
+        return w_recv.at[w % 2, i] if leaf else chain_recv.at[w % 2, i]
+
     def w_copies(h, w, i, targets):
         rows = pl.ds(pl.multiple_of(i * R, R), R)
         block = wn.at[h, w, rows, :]
@@ -310,7 +306,7 @@
 
         def copy(kind, dev):
             pltpu.make_async_remote_copy(
-                block, block, w_send.at[n, kind], s_recv.at[n] if kind == 2 else w_recv.at[n, i],
+                block, block, w_send.at[n, kind], arrival(w, kind == 3, i) if kind != 2 else s_recv.at[n],
                 device_id=dev, device_id_type=MESH).start()
 
         for kind, go, dev in targets:
@@ -329,12 +325,12 @@
             block, block, w_send.at[n, kind], s_recv.at[n],
             device_id=sibling, device_id_type=MESH)
 
-    def wait_block(h, w, i):
+    def wait_block(h, w, i, leaf):
         rows = pl.ds(pl.multiple_of(i * R, R), R)
         block = wn.at[h, w, rows, :]
         n = stream(h, w)
         pltpu.make_async_remote_copy(
-            block, block, w_send.at[n, 2], w_recv.at[n, i],
+            block, block, w_send.at[n, 2], arrival(w, leaf, i),
             device_id=sibling, device_id_type=MESH).wait_recv()
 
     is_owner = functools.reduce(jnp.logical_or, [owns(w) for w in range(3)])
@@ -342,9 +338,8 @@
 
     @pl.when(is_owner)
     def _():
-        wide = m_buf[...].astype(F32)
-        norm = jnp.sqrt(jnp.sum(wide * wide)) + 1e-07
-        m_buf[...] = (wide / norm).astype(BF16)
+        norm = jnp.sqrt(jnp.sum(square[...])) + 1e-07
+        m_buf[...] = (m_buf[...].astype(F32) / norm).astype(BF16)
         for step in range(NS_STEPS):
             x = m_buf[...]
             g_buf[...] = dot_nt(x, x).astype(BF16)
@@ -384,7 +379,7 @@
 
                 @pl.when(jnp.logical_and(live, jnp.logical_and(i >= 0, i < CHUNKS)))
                 def _():
-                    wait_block(h, w, i)
+                    wait_block(h, w, i, len(targets) == 1)
                     w_copies(h, w, i, targets)
 
             return 0
@@ -414,23 +409,21 @@
 
     loads[4].wait()
 
-    for kind in range(2):
-        token_wait(kind).wait_send()
-
-    @pl.when(pair)
+    token_wait(1).wait_send()
+
+    @pl.when(jnp.logical_or(jnp.logical_not(pair), middle))
+    def _():
+        token_wait(0).wait_send()
+
+    @pl.when(jnp.logical_and(pair, middle))
     def _():
         token_wait(2).wait_send()
 
     for w in range(3):
-        moved = jnp.logical_and(pair == (w < 2), z != owner_z(w, y))
-
-        @pl.when(jnp.logical_and(moved, jnp.logical_not(starts(w))) if w < 2 else moved)
-        def _():
-            chain_sent(w, 0).wait_send()
-
-        @pl.when(moved)
-        def _():
-            chain_sent(w, 1).wait_send()
+
+        @pl.when(jnp.logical_and(pair, z != owner_z(w, y)))
+        def _():
+            chain_sent(w).wait_send()
 
         @pl.when(pair == (w < 2))
         def _():
@@ -468,7 +461,6 @@
     D = fast_weights.shape[2]
     tokens = keys.shape[0]
     rows = tokens * 4
-    sums = D * D // (SUM_ROWS * SUM_COLS)
     vmem = pl.BlockSpec(memory_space=pltpu.VMEM)
     hbm = pl.BlockSpec(memory_space=pltpu.MemorySpace.HBM)
 
@@ -491,24 +483,24 @@
             pltpu.VMEM((rows, D), BF16),
             pltpu.VMEM((rows, D), BF16),
             pltpu.VMEM((2, rows, D), F32),
-            pltpu.VMEM((2, rows, D), BF16),
-            pltpu.VMEM((2, sums, SUM_ROWS, SUM_COLS), BF16),
-            pltpu.VMEM((2, sums, SUM_ROWS, SUM_COLS), BF16),
-            pltpu.VMEM((SUM_ROWS, SUM_COLS), F32),
+            pltpu.VMEM((3, rows, D), BF16),
+            pltpu.VMEM((3, D, D), F32),
+            pltpu.VMEM((3, SUM_CHUNKS, D // SUM_CHUNKS, D), BF16),
+            pltpu.VMEM((3, SUM_CHUNKS, D // SUM_CHUNKS, D), BF16),
+            pltpu.VMEM((D // SUM_CHUNKS, D), F32),
             pltpu.VMEM((D, D), BF16),
             pltpu.VMEM((D, D), F32),
             pltpu.VMEM((D, D), BF16),
             pltpu.VMEM((HEADS, 3, D, D), BF16),
             pltpu.SemaphoreType.DMA((3,)),
             pltpu.SemaphoreType.DMA((2, 4)),
-            pltpu.SemaphoreType.DMA((2, 2)),
-            pltpu.SemaphoreType.DMA((2, sums)),
+            pltpu.SemaphoreType.DMA((3,)),
+            pltpu.SemaphoreType.DMA((3, SUM_CHUNKS)),
             pltpu.SemaphoreType.DMA((4, 4)),
-            pltpu.SemaphoreType.DMA((4, CHUNKS)),
+            pltpu.SemaphoreType.DMA((2, CHUNKS)),
             pltpu.SemaphoreType.DMA((4,)),
             pltpu.SemaphoreType.DMA((1,)),
             pltpu.SemaphoreType.DMA((5,)),
-            pltpu.SemaphoreType.REGULAR,
         ],
         compiler_params=pltpu.CompilerParams(
             collective_id=0, has_side_effects=True, vmem_limit_bytes=30 * 1024 * 1024

time: 54.3 us -> 52 us (0.958)
  Pallas kernels: 53.5 us -> 51.2 us
    pallas_call x1, Pallas kernels: 51.8 us -> 49.4 us  [body(): pl.pallas_call(run, out_shape=(jax.ShapeDtypeStruct((tokens, HEADS * D),...]
where the time goes in v4:
time: 52 us; the launch traced here: 51.8 us
  Pallas kernels  51.2 us (98%)
  between operations  0.64 us (1%)
    pallas_call x1, Pallas kernels, body(): pl.pallas_call(run, out_shape=(jax.ShapeDtypeStruct((tokens, HEADS * D),...  49.4 us
    pallas_call x1, Pallas kernels, body(): pl.pallas_call(readout, out_shape=(jax.ShapeDtypeStruct(query.shape, BF16...  1.77 us

profile of v4, /device:TPU:0, one launch (start us, length us, event | category | flops | bytes accessed | tf_op | source)
XLA Modules:
  0.0 51.8 jit_solution(9501648494207445461)
XLA Ops:
  0.6 49.4 %ttt_step.1 = (bf16[128,1024]{1,0:T(8,128)(2,1)S(1)}, bf16[2,3,512,512]{3,2,1,0:T(8,128)(2,1)S(1)}) custom-call(bf16[128,1024]{1,0:T(8,128)(2,1)} %refs_0_.1, bf16[128,1024]{1,0:T(8,128)(2,1)} %refs_1_.1, bf16[128,1024]{1,0:T(8,128)(2,1)} %refs_2_.1, f32[2,128]{1,0:T(2,128)} %refs_3_.1, bf16[2,3,512,512]{3,2,1,0:T(8,128)(2,1)} %refs_4_.1), custom_call_target="tpu_custom_call" | custom-call | tf_op jit(solution)/shard_map/ttt_step/pallas_call | solution.py:470
  50.1 1.8 %readout.1 = (bf16[128,1024]{1,0:T(8,128)(2,1)}, bf16[2,3,512,512]{3,2,1,0:T(8,128)(2,1)}) custom-call(bf16[128,1024]{1,0:T(8,128)(2,1)S(1)} %get-tuple-element.4.query_ref, bf16[2,3,512,512]{3,2,1,0:T(8,128)(2,1)S(1)} %get-tuple-element.5.w_ref), custom_call_target="tpu_custom_call" | custom-call | tf_op jit(solution)/shard_map/readout/pallas_call | solution.py:510

commit v5 on v4

--- a/solution.py
+++ b/solution.py
@@ -8,12 +8,14 @@
 from jax.sharding import PartitionSpec as P
 
 HEADS = 2
-NS_STEPS = 2
+NS_BLOCKS = 4
 CHUNKS = 16
 SUM_CHUNKS = 16
 SUM_LAG = 7
 LAG = 6
 LEAF = 16
+LEAF_END = 8
+LATE = 6
 SHIFT = 0
 MESH = pl.DeviceIdType.MESH
 F32 = jnp.float32
@@ -37,7 +39,7 @@
     k_hbm, v_hbm, q_hbm, r_hbm, w_hbm,
     query_ref, neww_ref,
     v_ref, r_ref, w_ref,
-    o_loc, keys, outer, gates, grads, sums, recv, sendbuf, square, m_buf, x_buf, g_buf, wn,
+    o_loc, keys, outer, gates, grads, sums, recv, sendbuf, square, m_buf, x_buf, g_buf, mix_buf, wn,
     tok_send, tok_recv, chain_send, chain_recv, w_send, w_recv, s_recv, out_sem, in_sem,
 ):
     tokens = k_hbm.shape[0]
@@ -291,7 +293,7 @@
             return (leaf,)
         return (
             (0, jnp.logical_and(z >= own, z < Z - 1), {"tok": me + 4}),
-            (1, jnp.logical_and(z <= own, z > 0), {"tok": me - 4}),
+            (1, jnp.logical_and(z <= own, z > (1 if w == 1 else 0)), {"tok": me - 4}),
             (3, True, across),
             leaf,
         )
@@ -336,31 +338,43 @@
     is_owner = functools.reduce(jnp.logical_or, [owns(w) for w in range(3)])
     owned_w = jnp.where(owns(0), 0, jnp.where(owns(1), 1, 2))
 
+    def renew(i, targets):
+        rows = slice(i * R, (i + 1) * R)
+        old = w_ref[owned_w, rows, :].astype(F32)
+        fresh = old - m_buf[rows, :].astype(F32)
+        scale = jnp.sqrt(
+            (jnp.mean(old * old, axis=1, keepdims=True) + 1e-06)
+            / (jnp.mean(fresh * fresh, axis=1, keepdims=True) + 1e-06)
+        )
+        wn[y, owned_w, rows, :] = (fresh * scale).astype(BF16)
+        w_copies(y, owned_w, i, targets)
+
     @pl.when(is_owner)
     def _():
-        norm = jnp.sqrt(jnp.sum(square[...])) + 1e-07
-        m_buf[...] = (m_buf[...].astype(F32) / norm).astype(BF16)
-        for step in range(NS_STEPS):
-            x = m_buf[...]
-            g_buf[...] = dot_nt(x, x).astype(BF16)
+        scale = 1.0 / (jnp.sqrt(jnp.sum(square[...])) + 1e-07)
+
+        def mix(x_ref, factor):
+            x = x_ref[...]
+            g_buf[...] = (dot_nt(x, x) * factor).astype(BF16)
             g = g_buf[...]
-            mixed = (-4.775 * g.astype(F32) + 2.0315 * dot(g, g)).astype(BF16)
-            x_buf[...] = 3.4445 * x.astype(F32) + dot(mixed, x)
-            m_buf[...] = x_buf[...].astype(BF16)
+            mix_buf[...] = (-4.775 * g.astype(F32) + 2.0315 * dot(g, g)).astype(BF16)
+
+        mix(m_buf, scale * scale)
+        m = m_buf[...]
+        x_buf[...] = ((3.4445 * m.astype(F32) + dot(mix_buf[...], m)) * scale).astype(BF16)
+        mix(x_buf, 1.0)
         edges = (
             (0, z < Z - 1, {"tok": me + 4}), (1, z > 0, {"tok": me - 4}),
             (3, True, across), (2, True, sibling),
         )
-        for i in range(CHUNKS):
-            rows = slice(i * R, (i + 1) * R)
-            old = w_ref[owned_w, rows, :].astype(F32)
-            fresh = old - m_buf[rows, :].astype(F32)
-            scale = jnp.sqrt(
-                (jnp.mean(old * old, axis=1, keepdims=True) + 1e-06)
-                / (jnp.mean(fresh * fresh, axis=1, keepdims=True) + 1e-06)
-            )
-            wn[y, owned_w, rows, :] = (fresh * scale).astype(BF16)
-            w_copies(y, owned_w, i, edges)
+        step_rows = D // NS_BLOCKS
+        for b in range(NS_BLOCKS):
+            wide = slice(b * step_rows, (b + 1) * step_rows)
+            m_buf[wide, :] = (
+                3.4445 * x_buf[wide, :].astype(F32) + dot(mix_buf[wide, :], x_buf[...])
+            ).astype(BF16)
+            for i in range(b * CHUNKS // NS_BLOCKS, (b + 1) * CHUNKS // NS_BLOCKS):
+                renew(i, edges)
 
     def spread_all(ws):
         routes = []
@@ -368,18 +382,27 @@
         for home in (True, False):
             h = y if home else 1 - y
             for w in ws:
-                hops = jnp.abs(z - owner_z(w, h)) + (0 if home else 1)
-                start = LAG * (hops - 1) + (0 if home else LEAF)
-                routes.append((h, w, start, hops > 0, w_targets(w, home)))
+                away = jnp.abs(z - owner_z(w, h))
+                hops = away + (0 if home else 1)
+                edge = jnp.logical_or(z == 0, z == Z - 1)
+                start = LAG * jnp.maximum(away - 1, 0)
+                if not home:
+                    start = start + jnp.where(away > 0, jnp.where(edge, LEAF_END, LEAF), 0)
+                routes.append((h, w, start, hops > 0, True, w_targets(w, home), not home))
                 end = jnp.maximum(end, start + CHUNKS)
+                if home and w == 1:
+                    down = [(1, True, {"tok": me - 4})]
+                    routes.append((h, w, start + LATE, z == 1, False, down, False))
+                    end = jnp.maximum(end, start + LATE + CHUNKS)
 
         def step(t, _):
-            for h, w, start, live, targets in routes:
+            for h, w, start, live, waits, targets, leaf in routes:
                 i = t - start
 
                 @pl.when(jnp.logical_and(live, jnp.logical_and(i >= 0, i < CHUNKS)))
                 def _():
-                    wait_block(h, w, i, len(targets) == 1)
+                    if waits:
+                        wait_block(h, w, i, leaf)
                     w_copies(h, w, i, targets)
 
             return 0
@@ -429,7 +452,10 @@
         def _():
             for home in (True, False):
                 h = y if home else 1 - y
-                for kind, go, _ in w_targets(w, home):
+                targets = w_targets(w, home)
+                if home and w == 1:
+                    targets += ((1, z == 1, None),)
+                for kind, go, _ in targets:
 
                     @pl.when(go)
                     def _():
@@ -489,7 +515,8 @@
             pltpu.VMEM((3, SUM_CHUNKS, D // SUM_CHUNKS, D), BF16),
             pltpu.VMEM((D // SUM_CHUNKS, D), F32),
             pltpu.VMEM((D, D), BF16),
-            pltpu.VMEM((D, D), F32),
+            pltpu.VMEM((D, D), BF16),
+            pltpu.VMEM((D, D), BF16),
             pltpu.VMEM((D, D), BF16),
             pltpu.VMEM((HEADS, 3, D, D), BF16),
             pltpu.SemaphoreType.DMA((3,)),

time: 52 us -> 51.6 us (level)
  no operation moved by 1% of the time
where the time goes in v5:
time: 51.6 us; the launch traced here: 51.4 us
  Pallas kernels  50.8 us (98%)
  between operations  0.64 us (1%)
    pallas_call x1, Pallas kernels, body(): pl.pallas_call(run, out_shape=(jax.ShapeDtypeStruct((tokens, HEADS * D),...  49 us
    pallas_call x1, Pallas kernels, body(): pl.pallas_call(readout, out_shape=(jax.ShapeDtypeStruct(query.shape, BF16...  1.77 us

profile of v5, /device:TPU:0, one launch (start us, length us, event | category | flops | bytes accessed | tf_op | source)
XLA Modules:
  0.0 51.4 jit_solution(10441281261627866983)
XLA Ops:
  0.6 49.0 %ttt_step.1 = (bf16[128,1024]{1,0:T(8,128)(2,1)S(1)}, bf16[2,3,512,512]{3,2,1,0:T(8,128)(2,1)S(1)}) custom-call(bf16[128,1024]{1,0:T(8,128)(2,1)} %refs_0_.1, bf16[128,1024]{1,0:T(8,128)(2,1)} %refs_1_.1, bf16[128,1024]{1,0:T(8,128)(2,1)} %refs_2_.1, f32[2,128]{1,0:T(2,128)} %refs_3_.1, bf16[2,3,512,512]{3,2,1,0:T(8,128)(2,1)} %refs_4_.1), custom_call_target="tpu_custom_call" | custom-call | tf_op jit(solution)/shard_map/ttt_step/pallas_call | solution.py:496
  49.6 1.8 %readout.1 = (bf16[128,1024]{1,0:T(8,128)(2,1)}, bf16[2,3,512,512]{3,2,1,0:T(8,128)(2,1)}) custom-call(bf16[128,1024]{1,0:T(8,128)(2,1)S(1)} %get-tuple-element.4.query_ref, bf16[2,3,512,512]{3,2,1,0:T(8,128)(2,1)S(1)} %get-tuple-element.5.w_ref), custom_call_target="tpu_custom_call" | custom-call | tf_op jit(solution)/shard_map/readout/pallas_call | solution.py:537

commit v6 on v5

--- a/solution.py
+++ b/solution.py
@@ -156,18 +156,17 @@
             gate = dot(key, w_ref[0])
             upper = dot(key, w_ref[1])
 
-            gates[0, rows, :] = gate
-            gates[1, rows, :] = upper
-            grads[2, rows, :] = (gate * jax.nn.sigmoid(gate) * upper).astype(BF16)
+            sigma = jax.nn.sigmoid(gate)
+            silu_gate = gate * sigma
+            gates[0, rows, :] = upper * sigma * (1.0 + gate * (1.0 - sigma))
+            gates[1, rows, :] = silu_gate
+            grads[2, rows, :] = (silu_gate * upper).astype(BF16)
 
         @pl.when(jnp.logical_and(pair, s // 2 % 2 == 1))
         def _():
-            gate = gates[0, rows, :]
-            upper = gates[1, rows, :]
             back = dot_nt(outer[rows, :], w_ref[2])
-            sigma = jax.nn.sigmoid(gate)
-            grads[0, rows, :] = (back * upper * sigma * (1.0 + gate * (1.0 - sigma))).astype(BF16)
-            grads[1, rows, :] = (back * (gate * sigma)).astype(BF16)
+            grads[0, rows, :] = (back * gates[0, rows, :]).astype(BF16)
+            grads[1, rows, :] = (back * gates[1, rows, :]).astype(BF16)
 
         return 0
 
@@ -282,9 +281,6 @@
 
     def owns(w):
         return jnp.logical_and(pair == (w < 2), z == owner_z(w, y))
-
-    def stream(h, w):
-        return h * 2 + w % 2
 
     def w_targets(w, home):
         own = owner_z(w, y)
@@ -299,16 +295,16 @@
         )
 
     def arrival(w, leaf, i):
-        return w_recv.at[w % 2, i] if leaf else chain_recv.at[w % 2, i]
-
-    def w_copies(h, w, i, targets):
-        rows = pl.ds(pl.multiple_of(i * R, R), R)
+        return w_recv.at[w % 2, i // 2] if leaf else chain_recv.at[w % 2, i]
+
+    def w_copies(h, w, i, targets, size=1):
+        rows = pl.ds(pl.multiple_of(i * R, R), size * R)
         block = wn.at[h, w, rows, :]
-        n = stream(h, w)
 
         def copy(kind, dev):
             pltpu.make_async_remote_copy(
-                block, block, w_send.at[n, kind], arrival(w, kind == 3, i) if kind != 2 else s_recv.at[n],
+                block, block, w_send.at[kind],
+                arrival(w, kind == 3, i) if kind != 2 else s_recv.at[0],
                 device_id=dev, device_id_type=MESH).start()
 
         for kind, go, dev in targets:
@@ -320,19 +316,16 @@
                 def _():
                     copy(kind, dev)
 
-    def w_wait(h, w, kind):
-        block = wn.at[h, w]
-        n = stream(h, w)
+    def w_wait(block, kind):
         return pltpu.make_async_remote_copy(
-            block, block, w_send.at[n, kind], s_recv.at[n],
+            block, block, w_send.at[kind], s_recv.at[0],
             device_id=sibling, device_id_type=MESH)
 
-    def wait_block(h, w, i, leaf):
-        rows = pl.ds(pl.multiple_of(i * R, R), R)
+    def wait_block(h, w, i, leaf, size):
+        rows = pl.ds(pl.multiple_of(i * R, R), size * R)
         block = wn.at[h, w, rows, :]
-        n = stream(h, w)
         pltpu.make_async_remote_copy(
-            block, block, w_send.at[n, 2], arrival(w, leaf, i),
+            block, block, w_send.at[2], arrival(w, leaf, i),
             device_id=sibling, device_id_type=MESH).wait_recv()
 
     is_owner = functools.reduce(jnp.logical_or, [owns(w) for w in range(3)])
@@ -398,12 +391,16 @@
         def step(t, _):
             for h, w, start, live, waits, targets, leaf in routes:
                 i = t - start
-
-                @pl.when(jnp.logical_and(live, jnp.logical_and(i >= 0, i < CHUNKS)))
+                due = jnp.logical_and(i >= 0, i < CHUNKS)
+                if leaf:
+                    due = jnp.logical_and(due, i % 2 == 1)
+                size = 2 if leaf else 1
+
+                @pl.when(jnp.logical_and(live, due))
                 def _():
                     if waits:
-                        wait_block(h, w, i, leaf)
-                    w_copies(h, w, i, targets)
+                        wait_block(h, w, i - (size - 1), leaf, size)
+                    w_copies(h, w, i - (size - 1), targets, size)
 
             return 0
 
@@ -420,15 +417,23 @@
     def save(h, w):
         return pltpu.make_async_copy(wn.at[h, w], neww_ref.at[h, w], out_sem.at[0])
 
-    for mine_first in (True, False):
-        for w in range(3):
-
-            @pl.when((pair == (w < 2)) == mine_first)
-            def _():
-                for h in range(HEADS):
-                    if not mine_first:
-                        w_wait(h, w, 2).wait_recv()
-                    save(h, w).start()
+    def save_all(ws):
+        for w in ws:
+            for h in range(HEADS):
+                save(h, w).start()
+
+    def finish(own, others):
+        save_all(own)
+        w_wait(wn.at[:, others[0] : others[-1] + 1], 2).wait_recv()
+        save_all(others)
+
+    @pl.when(pair)
+    def _():
+        finish((0, 1), (2,))
+
+    @pl.when(jnp.logical_not(pair))
+    def _():
+        finish((2,), (0, 1))
 
     loads[4].wait()
 
@@ -448,18 +453,26 @@
         def _():
             chain_sent(w).wait_send()
 
-        @pl.when(pair == (w < 2))
-        def _():
-            for home in (True, False):
-                h = y if home else 1 - y
-                targets = w_targets(w, home)
-                if home and w == 1:
-                    targets += ((1, z == 1, None),)
-                for kind, go, _ in targets:
-
-                    @pl.when(go)
-                    def _():
-                        w_wait(h, w, kind).wait_send()
+    rise = jnp.where(pair, z < Z - 1, jnp.logical_and(z >= mid(y), z < Z - 1))
+    fall = jnp.where(pair, z > 0, jnp.logical_and(z <= mid(y), z > 0))
+
+    @pl.when(rise)
+    def _():
+        w_wait(wn.at[0, 0], 0).wait_send()
+
+    @pl.when(fall)
+    def _():
+        w_wait(wn.at[0, 0], 1).wait_send()
+
+    @pl.when(pair)
+    def _():
+        w_wait(wn.at[0, 0:2], 3).wait_send()
+        w_wait(wn.at[:, 0:2], 2).wait_send()
+
+    @pl.when(jnp.logical_not(pair))
+    def _():
+        w_wait(wn.at[0, 2], 3).wait_send()
+        w_wait(wn.at[:, 2:3], 2).wait_send()
 
     pltpu.make_async_copy(wn, neww_ref, out_sem.at[0]).wait()
 
@@ -523,9 +536,9 @@
             pltpu.SemaphoreType.DMA((2, 4)),
             pltpu.SemaphoreType.DMA((3,)),
             pltpu.SemaphoreType.DMA((3, SUM_CHUNKS)),
-            pltpu.SemaphoreType.DMA((4, 4)),
-            pltpu.SemaphoreType.DMA((2, CHUNKS)),
             pltpu.SemaphoreType.DMA((4,)),
+            pltpu.SemaphoreType.DMA((2, CHUNKS // 2)),
+            pltpu.SemaphoreType.DMA((1,)),
             pltpu.SemaphoreType.DMA((1,)),
             pltpu.SemaphoreType.DMA((5,)),
         ],

time: 51.6 us -> 51.4 us (level)
  no operation moved by 1% of the time
where the time goes in v6:
time: 51.4 us; the launch traced here: 51.2 us
  Pallas kernels  50.6 us (98%)
  between operations  0.64 us (1%)
    pallas_call x1, Pallas kernels, body(): pl.pallas_call(run, out_shape=(jax.ShapeDtypeStruct((tokens, HEADS * D),...  48.8 us
    pallas_call x1, Pallas kernels, body(): pl.pallas_call(readout, out_shape=(jax.ShapeDtypeStruct(query.shape, BF16...  1.77 us

profile of v6, /device:TPU:0, one launch (start us, length us, event | category | flops | bytes accessed | tf_op | source)
XLA Modules:
  0.0 51.2 jit_solution(7506171362503304093)
XLA Ops:
  0.6 48.8 %ttt_step.1 = (bf16[128,1024]{1,0:T(8,128)(2,1)S(1)}, bf16[2,3,512,512]{3,2,1,0:T(8,128)(2,1)S(1)}) custom-call(bf16[128,1024]{1,0:T(8,128)(2,1)} %refs_0_.1, bf16[128,1024]{1,0:T(8,128)(2,1)} %refs_1_.1, bf16[128,1024]{1,0:T(8,128)(2,1)} %refs_2_.1, f32[2,128]{1,0:T(2,128)} %refs_3_.1, bf16[2,3,512,512]{3,2,1,0:T(8,128)(2,1)} %refs_4_.1), custom_call_target="tpu_custom_call" | custom-call | tf_op jit(solution)/shard_map/ttt_step/pallas_call | solution.py:509
  49.4 1.8 %readout.1 = (bf16[128,1024]{1,0:T(8,128)(2,1)}, bf16[2,3,512,512]{3,2,1,0:T(8,128)(2,1)}) custom-call(bf16[128,1024]{1,0:T(8,128)(2,1)S(1)} %get-tuple-element.4.query_ref, bf16[2,3,512,512]{3,2,1,0:T(8,128)(2,1)S(1)} %get-tuple-element.5.w_ref), custom_call_target="tpu_custom_call" | custom-call | tf_op jit(solution)/shard_map/readout/pallas_call | solution.py:550

commit v7 on v6

--- a/solution.py
+++ b/solution.py
@@ -11,8 +11,8 @@
 NS_BLOCKS = 4
 CHUNKS = 16
 SUM_CHUNKS = 16
-SUM_LAG = 7
-LAG = 6
+SUM_LAG = 8
+LAG = 5
 LEAF = 16
 LEAF_END = 8
 LATE = 6

time: 51.4 us -> 51.4 us (level)
  no operation moved by 1% of the time
where the time goes in v7:
time: 51.4 us; the launch traced here: 51.2 us
  Pallas kernels  50.6 us (98%)
  between operations  0.64 us (1%)
    pallas_call x1, Pallas kernels, body(): pl.pallas_call(run, out_shape=(jax.ShapeDtypeStruct((tokens, HEADS * D),...  48.8 us
    pallas_call x1, Pallas kernels, body(): pl.pallas_call(readout, out_shape=(jax.ShapeDtypeStruct(query.shape, BF16...  1.77 us

profile of v7, /device:TPU:0, one launch (start us, length us, event | category | flops | bytes accessed | tf_op | source)
XLA Modules:
  0.0 51.2 jit_solution(12388644191652875900)
XLA Ops:
  0.6 48.8 %ttt_step.1 = (bf16[128,1024]{1,0:T(8,128)(2,1)S(1)}, bf16[2,3,512,512]{3,2,1,0:T(8,128)(2,1)S(1)}) custom-call(bf16[128,1024]{1,0:T(8,128)(2,1)} %refs_0_.1, bf16[128,1024]{1,0:T(8,128)(2,1)} %refs_1_.1, bf16[128,1024]{1,0:T(8,128)(2,1)} %refs_2_.1, f32[2,128]{1,0:T(2,128)} %refs_3_.1, bf16[2,3,512,512]{3,2,1,0:T(8,128)(2,1)} %refs_4_.1), custom_call_target="tpu_custom_call" | custom-call | tf_op jit(solution)/shard_map/ttt_step/pallas_call | solution.py:509
  49.4 1.8 %readout.1 = (bf16[128,1024]{1,0:T(8,128)(2,1)}, bf16[2,3,512,512]{3,2,1,0:T(8,128)(2,1)}) custom-call(bf16[128,1024]{1,0:T(8,128)(2,1)S(1)} %get-tuple-element.4.query_ref, bf16[2,3,512,512]{3,2,1,0:T(8,128)(2,1)S(1)} %get-tuple-element.5.w_ref), custom_call_target="tpu_custom_call" | custom-call | tf_op jit(solution)/shard_map/readout/pallas_call | solution.py:550

commit v8 on v6

--- a/solution.py
+++ b/solution.py
@@ -15,7 +15,7 @@
 LAG = 6
 LEAF = 16
 LEAF_END = 8
-LATE = 6
+LATE = 4
 SHIFT = 0
 MESH = pl.DeviceIdType.MESH
 F32 = jnp.float32
@@ -288,9 +288,9 @@
         if not home:
             return (leaf,)
         return (
+            (3, True, across),
             (0, jnp.logical_and(z >= own, z < Z - 1), {"tok": me + 4}),
             (1, jnp.logical_and(z <= own, z > (1 if w == 1 else 0)), {"tok": me - 4}),
-            (3, True, across),
             leaf,
         )
 
@@ -357,8 +357,8 @@
         x_buf[...] = ((3.4445 * m.astype(F32) + dot(mix_buf[...], m)) * scale).astype(BF16)
         mix(x_buf, 1.0)
         edges = (
-            (0, z < Z - 1, {"tok": me + 4}), (1, z > 0, {"tok": me - 4}),
-            (3, True, across), (2, True, sibling),
+            (3, True, across), (0, z < Z - 1, {"tok": me + 4}),
+            (1, z > 0, {"tok": me - 4}), (2, True, sibling),
         )
         step_rows = D // NS_BLOCKS
         for b in range(NS_BLOCKS):

time: 51.4 us -> 51.4 us (level)
  no operation moved by 1% of the time
where the time goes in v8:
time: 51.4 us; the launch traced here: 51.2 us
  Pallas kernels  50.6 us (98%)
  between operations  0.64 us (1%)
    pallas_call x1, Pallas kernels, body(): pl.pallas_call(run, out_shape=(jax.ShapeDtypeStruct((tokens, HEADS * D),...  48.8 us
    pallas_call x1, Pallas kernels, body(): pl.pallas_call(readout, out_shape=(jax.ShapeDtypeStruct(query.shape, BF16...  1.77 us

profile of v8, /device:TPU:0, one launch (start us, length us, event | category | flops | bytes accessed | tf_op | source)
XLA Modules:
  0.0 51.2 jit_solution(9926594323530435255)
XLA Ops:
  0.6 48.8 %ttt_step.1 = (bf16[128,1024]{1,0:T(8,128)(2,1)S(1)}, bf16[2,3,512,512]{3,2,1,0:T(8,128)(2,1)S(1)}) custom-call(bf16[128,1024]{1,0:T(8,128)(2,1)} %refs_0_.1, bf16[128,1024]{1,0:T(8,128)(2,1)} %refs_1_.1, bf16[128,1024]{1,0:T(8,128)(2,1)} %refs_2_.1, f32[2,128]{1,0:T(2,128)} %refs_3_.1, bf16[2,3,512,512]{3,2,1,0:T(8,128)(2,1)} %refs_4_.1), custom_call_target="tpu_custom_call" | custom-call | tf_op jit(solution)/shard_map/ttt_step/pallas_call | solution.py:509
  49.4 1.8 %readout.1 = (bf16[128,1024]{1,0:T(8,128)(2,1)}, bf16[2,3,512,512]{3,2,1,0:T(8,128)(2,1)}) custom-call(bf16[128,1024]{1,0:T(8,128)(2,1)S(1)} %get-tuple-element.4.query_ref, bf16[2,3,512,512]{3,2,1,0:T(8,128)(2,1)S(1)} %get-tuple-element.5.w_ref), custom_call_target="tpu_custom_call" | custom-call | tf_op jit(solution)/shard_map/readout/pallas_call | solution.py:550

commit v9 on v8

--- a/solution.py
+++ b/solution.py
@@ -8,11 +8,11 @@
 from jax.sharding import PartitionSpec as P
 
 HEADS = 2
-NS_BLOCKS = 4
+NS_BLOCKS = 8
 CHUNKS = 16
 SUM_CHUNKS = 16
 SUM_LAG = 7
-LAG = 6
+LAG = 5
 LEAF = 16
 LEAF_END = 8
 LATE = 4

time: 51.4 us -> 51.4 us (level)
  no operation moved by 1% of the time
where the time goes in v9:
time: 51.4 us; the launch traced here: 51.2 us
  Pallas kernels  50.6 us (98%)
  between operations  0.64 us (1%)
    pallas_call x1, Pallas kernels, body(): pl.pallas_call(run, out_shape=(jax.ShapeDtypeStruct((tokens, HEADS * D),...  48.8 us
    pallas_call x1, Pallas kernels, body(): pl.pallas_call(readout, out_shape=(jax.ShapeDtypeStruct(query.shape, BF16...  1.77 us

profile of v9, /device:TPU:0, one launch (start us, length us, event | category | flops | bytes accessed | tf_op | source)
XLA Modules:
  0.0 51.2 jit_solution(10364233368349308689)
XLA Ops:
  0.6 48.8 %ttt_step.1 = (bf16[128,1024]{1,0:T(8,128)(2,1)S(1)}, bf16[2,3,512,512]{3,2,1,0:T(8,128)(2,1)S(1)}) custom-call(bf16[128,1024]{1,0:T(8,128)(2,1)} %refs_0_.1, bf16[128,1024]{1,0:T(8,128)(2,1)} %refs_1_.1, bf16[128,1024]{1,0:T(8,128)(2,1)} %refs_2_.1, f32[2,128]{1,0:T(2,128)} %refs_3_.1, bf16[2,3,512,512]{3,2,1,0:T(8,128)(2,1)} %refs_4_.1), custom_call_target="tpu_custom_call" | custom-call | tf_op jit(solution)/shard_map/ttt_step/pallas_call | solution.py:509
  49.4 1.8 %readout.1 = (bf16[128,1024]{1,0:T(8,128)(2,1)}, bf16[2,3,512,512]{3,2,1,0:T(8,128)(2,1)}) custom-call(bf16[128,1024]{1,0:T(8,128)(2,1)S(1)} %get-tuple-element.4.query_ref, bf16[2,3,512,512]{3,2,1,0:T(8,128)(2,1)S(1)} %get-tuple-element.5.w_ref), custom_call_target="tpu_custom_call" | custom-call | tf_op jit(solution)/shard_map/readout/pallas_call | solution.py:550
